TPU v7x, 512 devices: a whole 4x4x16 slice. The times are simulated.
512 devices in a mesh: seq: 32 (over z, core), head: 16 (over x, y).
Axes of the slice: x: 4, y: 4, z: 16, core: 2. Of those that a mesh axis runs over, the one named last changes fastest.
Arguments:
- tokens: bfloat16 [2048, 3072], P(('seq', 'head')), may hold values from -6 to 6
- w_qkv: bfloat16 [3, 3072, 3072], P(None, 'head'), may hold values from -0.109375 to 0.109375
- lr_weight: bfloat16 [48, 3072], P('head'), may hold values from -0.21875 to 0.21875
- lr_base: float32 [48], P('head'), may hold values from 0.3 to 3
- conv_weight: float32 [2, 4, 3072], P(None, None, 'head'), may hold values from -3 to 3
- w_init: float32 [2, 48, 64, 64], P(None, 'head'), may hold values from -0.75 to 0.75
- w_out: bfloat16 [3072, 3072], P('head'), may hold values from -0.15625 to 0.15625
Outputs:
- mixed: bfloat16 [2048, 3072], P(('seq', 'head'))
All inputs are finite; a program needn't handle non-finite values.
Results may differ from a plain program's by a relative error of at most 0.018.
Values may be sent and summed in bfloat16 or wider, within the bound.
No kernel may reach another device: no remote copies, remote signals or barrier semaphores. Data moves between devices by JAX's collectives and lax.ppermute only.
A program may use at most 128 MiB of HBM per device.

v0:
```python
import jax
import jax.numpy as jnp
from jax import lax
from jax.sharding import PartitionSpec as P

MB = 16
KERNEL = 4


PRECISE = lax.Precision.HIGHEST
EPSILON = 1e-05


def from_behind(array, axis, by):
    length = lax.axis_size(axis)
    pairs = [(i, i + by) for i in range(length) if 0 <= i + by < length]
    return lax.ppermute(array, axis, pairs)


def entering(array, axis, combine, identity, reverse):
    length, index = (lax.axis_size(axis), lax.axis_index(axis))
    everything = jax.tree.map(lambda part: lax.all_gather(part, axis), array)
    start = jax.tree.map(
        lambda part, zero: jnp.broadcast_to(jnp.asarray(zero, part.dtype), part.shape),
        array,
        identity,
    )

    def lap(k, before):
        at = length - 1 - k if reverse else k
        reached = at > index if reverse else at < index
        new = combine(before, jax.tree.map(lambda part: part[at], everything))
        return jax.tree.map(lambda a, b: jnp.where(reached, a, b), new, before)

    return lax.fori_loop(0, length, lap, start)


def compose_maps(earlier_map, later_map):
    return (
        jnp.matmul(earlier_map[0], later_map[0], precision=PRECISE),
        jnp.matmul(earlier_map[1], later_map[0], precision=PRECISE) + later_map[1],
    )


def batch_terms(keys_unit, value_rows, step_rates):
    scaled = step_rates[..., None] * keys_unit
    identity_mat = jnp.eye(keys_unit.shape[-1], dtype=jnp.float32)
    transition = identity_mat - jnp.einsum(
        "...thc,...thd->...hcd", scaled, keys_unit, precision=PRECISE
    )
    offset = jnp.einsum("...thv,...thc->...hvc", value_rows, scaled, precision=PRECISE)
    return (transition, offset)


def batch_output(inner_state, queries, keys_unit, value_rows, step_rates, token_mask):
    applied_q = jnp.einsum("...hvc,...thc->...thv", inner_state, queries, precision=PRECISE)
    applied_k = jnp.einsum("...hvc,...thc->...thv", inner_state, keys_unit, precision=PRECISE)
    errors = applied_k - value_rows
    scores = jnp.einsum("...thc,...shc->...hts", queries, keys_unit, precision=PRECISE)
    scores = scores * token_mask * jnp.swapaxes(step_rates, -1, -2)[..., :, None, :]
    return applied_q - jnp.einsum("...hts,...shv->...thv", scores, errors, precision=PRECISE)


def layer_norm(inputs):
    average = jnp.mean(inputs, axis=-1, keepdims=True)
    centred = inputs - average
    variance = jnp.mean(centred * centred, axis=-1, keepdims=True)
    return centred / jnp.sqrt(variance + EPSILON)


def exclusive_maps(inclusive, identity_mat):
    transition = jnp.concatenate([identity_mat[None], inclusive[0][:-1]], axis=0)
    offset = jnp.concatenate([jnp.zeros_like(identity_mat)[None], inclusive[1][:-1]], axis=0)
    return (transition, offset)


def shards(tokens, w_qkv, lr_weight, lr_base, conv_weight, w_init, w_out):
    own_rows = tokens.shape[0]
    row_count = own_rows * lax.axis_size("head")
    inner_width = w_qkv.shape[1]
    head_count = lr_base.shape[0]
    head_size = w_init.shape[-1]
    batch_count = row_count // MB
    shard_piece = lax.all_gather(tokens, "head", axis=0, tiled=True)
    proj_piece = jnp.einsum("tn,cjn->ctj", shard_piece, w_qkv, preferred_element_type=jnp.float32)
    lr_piece = jnp.einsum("tn,hn->th", shard_piece, lr_weight, preferred_element_type=jnp.float32)
    projected = proj_piece.astype(jnp.bfloat16)
    rim_rows = KERNEL - 1
    previous = from_behind(projected[0:2, row_count - rim_rows :, :], "seq", 1)
    extended = jnp.concatenate([previous, projected[0:2]], axis=1).astype(jnp.float32)
    convolved = jnp.zeros((2, row_count, inner_width), jnp.float32)
    for position in range(KERNEL):
        convolved = (
            convolved
            + conv_weight[:, position][:, None, :] * extended[:, position : position + row_count, :]
        )
    queries = convolved[0].reshape(batch_count, MB, head_count, head_size)
    keys_conv = convolved[1].reshape(row_count, head_count, head_size)
    keys_unit = keys_conv / jnp.sqrt(
        (jnp.mean(keys_conv * keys_conv, axis=-1, keepdims=True) + EPSILON) * head_size
    )
    keys_unit = keys_unit.reshape(batch_count, MB, head_count, head_size)
    value_rows = projected[2].astype(jnp.float32).reshape(batch_count, MB, head_count, head_size)
    step_rates = (lr_base[None, :] * jax.nn.sigmoid(lr_piece) / MB).reshape(
        batch_count, MB, head_count
    )
    transition, offset = batch_terms(keys_unit, value_rows, step_rates)
    identity_mat = jnp.broadcast_to(
        jnp.eye(head_size, dtype=jnp.float32), (head_count, head_size, head_size)
    )
    fwd_incl = lax.associative_scan(compose_maps, (transition, offset), axis=0)
    rev_incl = lax.associative_scan(compose_maps, (transition[::-1], offset[::-1]), axis=0)
    fwd_excl = exclusive_maps(fwd_incl, identity_mat)
    rev_flip = exclusive_maps(rev_incl, identity_mat)
    rev_excl = (rev_flip[0][::-1], rev_flip[1][::-1])
    fwd_total = (fwd_incl[0][-1], fwd_incl[1][-1])
    rev_total = (rev_incl[0][-1], rev_incl[1][-1])
    fwd_prior = entering(
        (fwd_total[0], fwd_total[1]),
        "seq",
        compose_maps,
        (identity_mat, jnp.zeros_like(identity_mat)),
        False,
    )
    rev_prior = entering(
        (rev_total[0], rev_total[1]),
        "seq",
        compose_maps,
        (identity_mat, jnp.zeros_like(identity_mat)),
        True,
    )
    fwd_start = jnp.matmul(w_init[0], fwd_prior[0], precision=PRECISE) + fwd_prior[1]
    rev_start = jnp.matmul(w_init[1], rev_prior[0], precision=PRECISE) + rev_prior[1]
    fwd_states = jnp.matmul(fwd_start[None], fwd_excl[0], precision=PRECISE) + fwd_excl[1]
    rev_states = jnp.matmul(rev_start[None], rev_excl[0], precision=PRECISE) + rev_excl[1]
    causal_mask = (jnp.arange(MB)[:, None] >= jnp.arange(MB)[None, :]).astype(jnp.float32)
    anti_mask = jnp.transpose(causal_mask)
    fwd_out = batch_output(fwd_states, queries, keys_unit, value_rows, step_rates, causal_mask)
    rev_out = batch_output(rev_states, queries, keys_unit, value_rows, step_rates, anti_mask)
    hidden = (
        (layer_norm(fwd_out) + layer_norm(rev_out))
        .reshape(row_count, inner_width)
        .astype(jnp.bfloat16)
    )
    partial_out = jnp.dot(hidden, w_out, preferred_element_type=jnp.float32)
    summed = lax.psum_scatter(
        partial_out.astype(jnp.bfloat16), "head", scatter_dimension=0, tiled=True
    )
    return summed


def solution(mesh):
    placed = (
        P(("seq", "head"), None),
        P(None, "head", None),
        P("head", None),
        P("head"),
        P(None, None, "head"),
        P(None, "head", None, None),
        P("head", None),
    )
    return jax.shard_map(
        shards, mesh=mesh, in_specs=placed, out_specs=P(("seq", "head"), None), check_vma=False
    )
```

profile of v0, /device:TPU:1, one launch (start us, length us, event | category | flops | bytes accessed | tf_op | source)
XLA Modules:
  0.0 929.4 jit_solution(15973213649660845457)
XLA Ops:
  6.5 22.8 %all-gather = bf16[16,4,3072]{2,1,0:T(4,128)(2,1)} all-gather(bf16[1,4,3072]{2,1,0:T(4,128)(2,1)} %bitcast.216), channel_id=1, replica_groups=mesh['seq'=32,'head'=16] {'head'}, dimensions={0}, use_global_device_ids=true | all-gather | bytes 417792 | tf_op jit(solution)/shard_map/all_gather | solution.py:84
  31.2 2.3 fusion.28
  34.7 9.0 collective-permute-start
  68.6 4.3 pad.61
  74.5 4.3 pad.60
  83.9 4.3 pad.57
  91.6 4.3 pad.56
  110.9 4.3 pad.166
  118.0 4.3 pad.68
  127.3 4.2 pad.90
  131.5 4.3 pad.88
  140.7 4.2 pad.92
  144.9 4.3 pad.64
  149.1 4.2 pad.94
  156.6 4.3 pad.65
  166.1 2.0 fusion.84
  173.8 53.1 %all-gather.6.cloned.1.call-done = f32[32,3,64,64]{3,2,1,0:T(8,128)} async-done(((f32[1,3,64,64]{3,2,1,0:T(8,128)}), f32[32,3,64,64]{3,2,1,0:T(8,128)}) %all-gather.6.cloned.1.call-update) | async-done | bytes 1572880 | tf_op jit(solution)/shard_map/all_gather | solution.py:22
  228.3 279.4 %while.34 = (s32[]{:T(128)}, f32[3,64,64]{1,2,0:T(8,128)}, f32[3,64,64]{1,2,0:T(8,128)}, s32[]{:T(128)}, f32[32,3,64,64]{3,2,1,0:T(8,128)}, /*index=5*/f32[32,3,64,64]{3,2,1,0:T(8,128)}, s32[]{:T(128)}, s32[]{:T(128)}) while((s32[]{:T(128)}, f32[3,64,64]{1,2,0:T(8,128)}, f32[3,64,64]{1,2,0:T(8,128)}, s32[]{:T(128)}, ...), condition=%wide.region_2.3_spmd.clone, body=%wide.region_1.2_spmd.clone.sunk | while | flops 18935812 | bytes 1182316 | solution.py:35
  267.2 1.9 fusion.154
  511.9 2.3 convolution_bitcast_fusion.21
  514.1 2.3 fusion.36
  517.9 279.9 %while.35 = (s32[]{:T(128)}, f32[3,64,64]{1,2,0:T(8,128)}, f32[3,64,64]{1,2,0:T(8,128)}, s32[]{:T(128)}, f32[32,3,64,64]{3,2,1,0:T(8,128)}, /*index=5*/f32[32,3,...) while((s32[]{:T(128)}, f32[3,64,64]{1,2,0:T(8,128)}, f32[3,64,64]{1,2,0:T(8,128)}, ...), condition=%wide.region_6.7_spmd.clone, body=%wide.region_5.6_spmd.clone.sunk | while | flops 18935816 | bytes 1181870 | solution.py:35
  808.6 2.4 convolution_convert_fusion
  813.0 108.5 %all-reduce.21.cloned.1.call-done = bf16[64,3072]{1,0:T(8,128)(2,1)} async-done(((bf16[64,3072]{1,0:T(8,128)(2,1)}), bf16[64,3072]{1,0:T(8,128)(2,1)}) %all-reduce.21.cloned.1.call-update) | async-done | bytes 393232
  (527 shorter events, 657.4 us)
Async XLA Ops:
  6.5 24.6 %copy-start = (bf16[3,192,3072]{2,1,0:T(8,128)(2,1)S(1)}, bf16[3,192,3072]{2,1,0:T(8,128)(2,1)}, u32[]{:S(2)}) copy-start(bf16[3,192,3072]{2,1,0:T(8,128)(2,1)} %param.12) | copy-start | bytes 10616836
  6.5 167.2 %all-gather.8.cloned.1.call-start = ((), (), s32[]{:S(2)}) async-start(), calls=%async_computation.1 | async-start | bytes 3244032 | tf_op jit(solution)/shard_map/all_gather | solution.py:22
  31.2 14.3 %copy-start.16 = (f32[2,4,192]{2,1,0:T(4,128)S(1)}, f32[2,4,192]{2,1,0:T(4,128)}, u32[]{:S(2)}) copy-start(f32[2,4,192]{2,1,0:T(4,128)} %param.15) | copy-start | bytes 18436
  31.2 14.9 %copy-start.17 = (f32[3]{0:T(128)S(1)}, f32[3]{0:T(128)}, u32[]{:S(2)}) copy-start(f32[3]{0:T(128)} %param.14) | copy-start | bytes 40
  33.4 0.6 copy-start.12
  34.7 19.5 %collective-permute-start = (bf16[2,3,192]{2,1,0:T(4,128)(2,1)}, bf16[2,3,192]{2,1,0:T(4,128)(2,1)}, u32[]{:S(2)}, u32[]{:S(2)}) collective-permute-start(bf16[2,3,192]{2,1,0:T(4,128)(2,1)} %slice.228), channel_id=1, source_target_pairs={{0,16},{16,32},{32,48},{48,64},{64,80},{80,96},{96,112},{112,128},... | collective-permute-start | bytes 6920 | tf_op jit(solution)/shard_map/ppermute | solution.py:17
  52.1 16.5 %copy-start.14 = (f32[4,16,3]{1,0,2:T(4,128)}, f32[4,16,3]{1,0,2:T(4,128)S(1)}, u32[]{:S(2)}) copy-start(f32[4,16,3]{1,0,2:T(4,128)S(1)} %mul.127) | copy-start | bytes 2308
  63.8 3.2 copy-start.1
  65.4 2.5 copy-start.2
  65.7 2.2 copy-start.4
  80.4 146.5 %all-gather.6.cloned.1.call-start = ((), (), s32[]{:S(2)}) async-start(), calls=%async_computation | async-start | bytes 3244032 | tf_op jit(solution)/shard_map/all_gather | solution.py:22
  81.3 1.2 copy-start.7
  82.5 0.6 copy-start.9
  97.5 419.0 %all-gather.12.cloned.1.call-start = ((), (), s32[]{:S(2)}) async-start(), calls=%async_computation.3 | async-start | bytes 3244032 | tf_op jit(solution)/shard_map/all_gather | solution.py:22
  107.3 2.3 copy-start.10
  108.6 0.7 copy-start.3
  109.6 0.6 copy-start.11
  123.9 392.6 %all-gather.10.cloned.1.call-start = ((), (), s32[]{:S(2)}) async-start(), calls=%async_computation.2 | async-start | bytes 3244032 | tf_op jit(solution)/shard_map/all_gather | solution.py:22
  136.7 1.2 copy-start.6
  137.9 1.2 copy-start.8
  173.5 747.9 %all-reduce.21.cloned.1.call-start = ((), (), s32[]{:S(2)}) async-start(), calls=%async_computation.4 | async-start | bytes 786432
  509.7 0.6 copy-start.5
  797.8 7.9 copy-start.13
  797.8 7.9 copy-start.15
Sparse Core Ops, SparseCore 0:
  80.5 73.8 all-gather.7
  156.5 70.3 all-gather.5
  229.0 70.0 all-gather.11
  301.0 70.0 all-gather.9
  811.2 110.2 all-reduce.20
where the time goes:
time: 948 us; the launch traced here: 929 us
  local copies, waits for them, and re-layouts  413 us (44%)
  matrix products  281 us (30%)
  waiting for transfers between devices  162 us (17%)
  other arithmetic  27.7 us (3%)
  blocking collectives  22.8 us (2%)
  between operations  14.2 us (1%)
    dynamic_slice x128, local copies, waits for them, and re-layouts, lap(): new = combine(before, jax.tree.map(lambda part: part[at], everything))  202 us
    dot_general x70, matrix products, compose_maps(): jnp.matmul(earlier_map[1], later_map[0], precision=PRECISE) + later_map[1]  127 us
    dot_general x70, matrix products, compose_maps(): jnp.matmul(earlier_map[0], later_map[0], precision=PRECISE)  127 us
    while x128, local copies, waits for them, and re-layouts  114 us
    unnamed x6, waiting for transfers between devices  109 us
    all_gather x4, waiting for transfers between devices, entering(): everything = jax.tree.map(lambda part: lax.all_gather(part, axis), array)  53.1 us
    all_gather x1, blocking collectives, shards(): shard_piece = lax.all_gather(tokens, 'head', axis=0, tiled=True)  22.8 us
  transfers between devices with their start and end apart: 6, of which 2 were waited for; matrix products, arithmetic and copies ran while one was open for 42% of the time, Pallas kernels for 0%

commit v1 on v0

v1 whole, which is shorter than its diff:
```python
import jax
import jax.numpy as jnp
from jax import lax
from jax.experimental import pallas as pl
from jax.experimental.pallas import tpu as pltpu
from jax.sharding import PartitionSpec as P

MB = 16
KERNEL = 4
EPSILON = 1e-05
F32 = jnp.float32
BF16 = jnp.bfloat16


def mm(a, b, ca=1, cb=0):
    return lax.dot_general(a, b, (((ca,), (cb,)), ((), ())), preferred_element_type=F32)


def local_kernel(own_ref, mate_ref, halo0_ref, halo1_ref, w_ref, lrw_ref, base_ref, taps_ref,
                 maps_ref, qeff_ref, oeff_ref, xall_ref, wide_ref, lrp_ref):
    core = lax.axis_index("seq") % 2
    half = w_ref.shape[2] // 2
    tokens = own_ref.shape[0] // 2

    def spread(src, row, count):
        for j in range(half // 128):
            wide_ref[j, 0:2 * count, :] = src[:, j * 128:(j + 1) * 128].astype(F32)
            for part in range(2):
                xall_ref[pl.ds(row, count), part * half + j * 128:part * half + (j + 1) * 128] = (
                    wide_ref[j, pl.ds(part, count, stride=2), :].astype(BF16))

    spread(own_ref[...], pl.multiple_of(core * tokens, 64), tokens)
    spread(mate_ref[...], pl.multiple_of((1 - core) * tokens, 64), tokens)
    halo = jnp.where(core == 0, halo0_ref[...].astype(F32), halo1_ref[...].astype(F32))
    for j in range(half // 128):
        wide_ref[j, 0:8, :] = halo[:, j * 128:(j + 1) * 128]
        for part in range(2):
            xall_ref[128:144, part * half + j * 128:part * half + (j + 1) * 128] = (
                wide_ref[j, pl.ds(part, 16, stride=2), :].astype(BF16))
    lrp_ref[...] = jnp.zeros_like(lrp_ref)
    lrp_ref[0:3, :] = lrw_ref[...]

    inner = w_ref.shape[1]
    rows = jnp.concatenate([w_ref[...].reshape(3 * inner, 2 * half), lrp_ref[...]], axis=0)
    proj = mm(rows, xall_ref[0:256, :], 1, 1)

    lane = lax.broadcasted_iota(jnp.int32, (2 * inner, 128), 1)
    qk = proj[0:2 * inner, 0:128].astype(BF16).astype(F32)
    edge = proj[0:2 * inner, 128:256].astype(BF16).astype(F32)
    taps = taps_ref[...]
    conv = taps[:, KERNEL - 1:KERNEL] * qk
    for back in range(1, KERNEL):
        moved = jnp.where(lane < back, pltpu.roll(edge, (back - 4) % 128, 1), pltpu.roll(qk, back, 1))
        conv = conv + taps[:, KERNEL - 1 - back:KERNEL - back] * moved
    values = proj[2 * inner:3 * inner, 0:128].astype(BF16)
    gate = jax.nn.sigmoid(proj[3 * inner:3 * inner + 8, 0:128])

    sign = 1 - 2 * core
    src = lax.broadcasted_iota(jnp.int32, (128, 128), 0)
    dst = lax.broadcasted_iota(jnp.int32, (128, 128), 1)
    seen = sign * (dst - src) >= 0
    strict = sign * (dst // MB - src // MB) > 0
    eye = jnp.where(src == dst, 1.0, 0.0).astype(F32)

    heads = inner // 64
    for h in range(heads):
        lo, hi = h * 64, (h + 1) * 64
        q = conv[lo:hi]
        k = conv[inner + lo:inner + hi]
        k = k * lax.rsqrt((jnp.mean(k * k, axis=0, keepdims=True) + EPSILON) * 64)
        rate = gate[h:h + 1] * (base_ref[h] / MB)
        kb = k.astype(BF16)
        krb = (k * rate).astype(BF16)
        krt = krb.T
        v = values[lo:hi]
        grams = mm(krt, jnp.concatenate([kb, q.astype(BF16)], axis=1))
        u = jnp.where(strict, grams[:, 0:128], 0.0)
        s = jnp.where(seen, grams[:, 128:256], 0.0)
        ub = u.astype(BF16)
        u2 = mm(ub, ub)
        u2b = u2.astype(BF16)
        u4 = mm(u2b, u2b)
        t1 = eye - u + u2 - mm(ub, u2b)
        t = t1 + mm(t1.astype(BF16), u4.astype(BF16))
        solved = mm(t.astype(BF16), jnp.concatenate([s.astype(BF16), krt], axis=1)).astype(BF16)
        both = mm(jnp.concatenate([kb, v], axis=0), solved)
        maps_ref[lo:hi, :] = jnp.concatenate([-both[0:64, 128:192], both[64:128, 128:192]], axis=1).astype(BF16)
        qeff_ref[lo:hi, :] = (q - both[0:64, 0:128]).astype(BF16)
        oeff_ref[lo:hi, :] = both[64:128, 0:128]


def chain_kernel(maps_ref, qeff_ref, oeff_ref, init_ref, out_ref):
    place = lax.axis_index("seq")
    core = place % 2
    chip = place // 2
    chips = maps_ref.shape[0]
    steps = jnp.where(core == 0, chip, chips - 1 - chip)
    heads = init_ref.shape[1]
    states = [init_ref[core, h] for h in range(heads)]
    for i in range(chips - 1):
        at = jnp.where(core == 0, i, chips - 1 - i)
        live = i < steps
        for h in range(heads):
            block = maps_ref[at, h * 64:(h + 1) * 64, :]
            new = states[h] + mm(states[h].astype(BF16), block[:, 0:64]) + block[:, 64:128].astype(F32)
            states[h] = jnp.where(live, new, states[h])
    for h in range(heads):
        lo, hi = h * 64, (h + 1) * 64
        out = mm(states[h].astype(BF16), qeff_ref[lo:hi, :]) + oeff_ref[lo:hi, :]
        centred = out - jnp.mean(out, axis=0, keepdims=True)
        variance = jnp.mean(centred * centred, axis=0, keepdims=True)
        out_ref[lo:hi, :] = centred * lax.rsqrt(variance + EPSILON)


def project_kernel(own_ref, mate_ref, w_ref, out_ref):
    core = lax.axis_index("seq") % 2
    hidden = (own_ref[...] + mate_ref[...]).astype(BF16)
    row = lax.broadcasted_iota(jnp.int32, (128, 128), 0)
    col = lax.broadcasted_iota(jnp.int32, (128, 128), 1)
    pick = jnp.where(col == row // 2 + 64 * core, 1.0, 0.0).astype(BF16)
    twice = mm(pick, hidden, 1, 1).astype(BF16)
    half = out_ref.shape[1]
    even = lax.broadcasted_iota(jnp.int32, (128, half), 0) % 2 == 0
    first = mm(twice, w_ref[:, 0:half])
    second = mm(twice, w_ref[:, half:2 * half])
    out_ref[...] = jnp.where(even, first, second).astype(BF16)


def total_kernel(parts_ref, out_ref, wide_ref):
    acc = parts_ref[0].astype(F32)
    for i in range(1, parts_ref.shape[0]):
        acc = acc + parts_ref[i].astype(F32)
    half = acc.shape[1]
    for j in range(half // 128):
        wide_ref[j] = acc[:, j * 128:(j + 1) * 128]
        for part in range(2):
            out_ref[:, part * half + j * 128:part * half + (j + 1) * 128] = (
                wide_ref[j, pl.ds(part, 4, stride=2), :].astype(BF16))


def shards(tokens, w_qkv, lr_weight, lr_base, conv_weight, w_init, w_out):
    width = tokens.shape[1]
    half = width // 2
    inner = w_qkv.shape[1]
    n_seq = lax.axis_size("seq")
    n_head = lax.axis_size("head")
    params = pltpu.CompilerParams(vmem_limit_bytes=48 * 1024 * 1024)
    vmem = pl.BlockSpec(memory_space=pltpu.VMEM)
    smem = pl.BlockSpec(memory_space=pltpu.SMEM)

    folded = jnp.broadcast_to(tokens.reshape(1, 8, half), (n_head, 8, half))
    own = lax.all_to_all(folded, "head", 0, 0)
    swap = [(i, i ^ 1) for i in range(n_seq)]
    mate = lax.ppermute(own, "seq", swap)
    tail = own[n_head - 1]
    halo0 = lax.ppermute(tail, "seq", [(i, i + 1) for i in range(1, n_seq - 1, 2)])
    halo1 = lax.ppermute(tail, "seq", [(i, i + 2) for i in range(1, n_seq - 2, 2)])
    taps = jnp.transpose(conv_weight, (0, 2, 1)).reshape(2 * inner, KERNEL)

    maps, qeff, oeff = pl.pallas_call(
        local_kernel,
        out_shape=(
            jax.ShapeDtypeStruct((inner, 128), BF16),
            jax.ShapeDtypeStruct((inner, 128), BF16),
            jax.ShapeDtypeStruct((inner, 128), F32),
        ),
        in_specs=[vmem, vmem, vmem, vmem, vmem, vmem, smem, vmem],
        out_specs=(vmem, vmem, vmem),
        scratch_shapes=[
            pltpu.VMEM((256, width), BF16),
            pltpu.VMEM((half // 128, 128, 128), F32),
            pltpu.VMEM((16, width), BF16),
        ],
        compiler_params=params,
        name="local",
    )(own.reshape(n_head * 8, half), mate.reshape(n_head * 8, half), halo0, halo1, w_qkv, lr_weight, lr_base, taps)

    groups = [list(range(c, n_seq, 2)) for c in range(2)]
    gathered = lax.all_gather(maps, "seq", axis_index_groups=groups)
    normed = pl.pallas_call(
        chain_kernel,
        out_shape=jax.ShapeDtypeStruct((inner, 128), F32),
        in_specs=[vmem] * 4,
        out_specs=vmem,
        compiler_params=params,
        name="chain",
    )(gathered, qeff, oeff, w_init)
    other = lax.ppermute(normed, "seq", swap)
    partial = pl.pallas_call(
        project_kernel,
        out_shape=jax.ShapeDtypeStruct((n_head * 8, half), BF16),
        in_specs=[vmem] * 3,
        out_specs=vmem,
        compiler_params=params,
        name="project",
    )(normed, other, w_out)
    parts = lax.all_to_all(partial.reshape(n_head, 8, half), "head", 0, 0)
    return pl.pallas_call(
        total_kernel,
        out_shape=jax.ShapeDtypeStruct(tokens.shape, BF16),
        in_specs=[vmem],
        out_specs=vmem,
        scratch_shapes=[pltpu.VMEM((half // 128, 8, 128), F32)],
        compiler_params=params,
        name="total",
    )(parts)


def solution(mesh):
    placed = (
        P(("seq", "head"), None),
        P(None, "head", None),
        P("head", None),
        P("head"),
        P(None, None, "head"),
        P(None, "head", None, None),
        P("head", None),
    )
    return jax.shard_map(
        shards, mesh=mesh, in_specs=placed, out_specs=P(("seq", "head"), None), check_vma=False
    )
```

time: 948 us -> 95 us (0.10); the launches traced: 929 us -> 94.6 us
  local copies, waits for them, and re-layouts: 413 us -> 5.05 us
  matrix products: 281 us -> 0 us
  waiting for transfers between devices: 162 us -> 1.01 us
  blocking collectives: 22.8 us -> 60.4 us
  other arithmetic: 27.7 us -> 0 us
  between operations: 14.2 us -> 0.1 us
  starting transfers between devices: 9.33 us -> 20.2 us
    dot_general x156 -> x0, matrix products: 281 us -> none  [the longest x70 127 us: compose_maps(): jnp.matmul(earlier_map[1], later_map[0], precision=PRECISE) + later_map[1]]
    dynamic_slice x128 -> x0, local copies, waits for them, and re-layouts: 202 us -> none  [lap(): new = combine(before, jax.tree.map(lambda part: part[at], everything))]
    while x128 -> x0, local copies, waits for them, and re-layouts: 114 us -> none
    unnamed x6 -> x0, waiting for transfers between devices: 109 us -> none
    all_gather x4 -> x0, waiting for transfers between devices: 53.1 us -> none  [entering(): everything = jax.tree.map(lambda part: lax.all_gather(part, axis), array)]
    slice x19 -> x0, local copies, waits for them, and re-layouts: 32.7 us -> none  [the longest x2 8.49 us: exclusive_maps(): inclusive[0][:-1]]
    pad x7 -> x0, local copies, waits for them, and re-layouts: 29.9 us -> none  [the longest x4 17.1 us: shards(): fwd_incl = lax.associative_scan(compose_maps, (transition, offset), axis=0)]
    all_to_all x0 -> x2, blocking collectives: none -> 28 us  [the longest x1 15.5 us: shards(): own = lax.all_to_all(folded, 'head', 0, 0)]
  transfers between devices with their start and end apart: 6 -> 4, of which waited for: 2 -> 2; matrix products, arithmetic and copies ran while one was open for 42% -> 1% of each run, Pallas kernels for 0% -> 0%
where the time goes in v1:
time: 95 us; the launch traced here: 94.6 us
  blocking collectives  60.4 us (64%)
  starting transfers between devices  20.2 us (21%)
  Pallas kernels  7.86 us (8%)
  local copies, waits for them, and re-layouts  5.05 us (5%)
  waiting for transfers between devices  1.01 us (1%)
    all_gather x1, blocking collectives, shards(): gathered = lax.all_gather(maps, 'seq', axis_index_groups=groups)  32.4 us
    all_to_all x1, blocking collectives, shards(): own = lax.all_to_all(folded, 'head', 0, 0)  15.5 us
    all_to_all x1, blocking collectives, shards(): parts = lax.all_to_all(partial.reshape(n_head, 8, half), 'head', 0, 0)  12.5 us
    ppermute x1, starting transfers between devices, shards(): other = lax.ppermute(normed, 'seq', swap)  10.7 us
    ppermute x1, starting transfers between devices, shards(): mate = lax.ppermute(own, 'seq', swap)  5.13 us
    pallas_call x1, Pallas kernels, shards(): pl.pallas_call(local_kernel, out_shape=(jax.ShapeDtypeStruct((inner, 128)...  4.6 us
    unnamed x10, local copies, waits for them, and re-layouts  3.4 us
    ppermute x1, starting transfers between devices, shards(): lax.ppermute(tail, 'seq', [(i, i + 2) for i in range(1, n_seq - 2, 2)])  3.11 us
  transfers between devices with their start and end apart: 4, of which 2 were waited for; matrix products, arithmetic and copies ran while one was open for 1% of the time, Pallas kernels for 0%

profile of v1, /device:TPU:1, one launch (start us, length us, event | category | flops | bytes accessed | tf_op | source)
XLA Modules:
  0.0 94.6 jit_solution(12195994675721443900)
XLA Ops:
  0.0 0.0 copy-start.2
  0.0 0.8 broadcast_in_dim.7
  0.8 0.0 copy-start.1
  0.8 15.5 %all_to_all.10 = bf16[16,8,1536]{2,1,0:T(8,128)(2,1)S(1)} all-to-all(bf16[16,8,1536]{2,1,0:T(8,128)(2,1)S(1)} %broadcast_in_dim.8), channel_id=1, replica_groups=mesh['seq'=32,'head'=16] {'head'}, dimensions={0} | all-to-all | bytes 786432 | tf_op jit(solution)/shard_map/all_to_all | solution.py:152
  16.3 5.1 %collective-permute-start = (bf16[16,8,1536]{2,1,0:T(8,128)(2,1)S(1)}, bf16[16,8,1536]{2,1,0:T(8,128)(2,1)S(1)}, u32[]{:S(2)}, u32[]{:S(2)}) collective-permute-start(bf16[16,8,1536]{2,1,0:T(8,128)(2,1)S(1)} %all_to_all.10), channel_id=1, source_target_pairs={{0,16},{16,0},{32,48},{48,32},{64,80},{80,64},{96,112},{112,96},{1... | collective-permute-start | bytes 1179656 | tf_op jit(solution)/shard_map/ppermute | solution.py:154
  21.5 3.1 %collective-permute-start.2 = (bf16[8,1536]{1,0:T(8,128)(2,1)S(1)}, bf16[8,1536]{1,0:T(8,128)(2,1)S(1)}, u32[]{:S(2)}, u32[]{:S(2)}) collective-permute-start(bf16[8,1536]{1,0:T(8,128)(2,1)S(1)} %slice_bitcast_fusion), channel_id=1, source_target_pairs={{16,48},{48,80},{80,112},{112,144},{144,176},{176,208},{208,240},{... | collective-permute-start | bytes 73736 | tf_op jit(solution)/shard_map/ppermute | solution.py:157
  24.6 1.3 %collective-permute-start.1 = (bf16[8,1536]{1,0:T(8,128)(2,1)S(1)}, bf16[8,1536]{1,0:T(8,128)(2,1)S(1)}, u32[]{:S(2)}, u32[]{:S(2)}) collective-permute-start(bf16[8,1536]{1,0:T(8,128)(2,1)S(1)} %slice_bitcast_fusion), channel_id=1, source_target_pairs={{16,32},{48,64},{80,96},{112,128},{144,160},{176,192},{208,224},{2... | collective-permute-start | bytes 73736 | tf_op jit(solution)/shard_map/ppermute | solution.py:156
  25.9 0.8 copy.8
  26.7 0.0 collective-permute-done.2.halo1_ref
  26.7 0.1 collective-permute-done.1.halo0_ref
  26.8 0.0 collective-permute-done
  26.8 2.0 %copy-done = bf16[3,192,3072]{2,1,0:T(8,128)(2,1)S(1)} copy-done((bf16[3,192,3072]{2,1,0:T(8,128)(2,1)S(1)}, bf16[3,192,3072]{2,1,0:T(8,128)(2,1)}, u32[]{:S(2)}) %copy-start) | copy-done | bytes 3538968
  28.8 0.7 copy-done.3
  29.6 0.7 copy-done.4
  30.2 4.6 %local.1 = (bf16[192,128]{1,0:T(8,128)(2,1)S(1)}, bf16[192,128]{1,0:T(8,128)(2,1)S(1)}, f32[192,128]{1,0:T(8,128)S(1)}) custom-call(bf16[128,1536]{1,0:T(8,128)(2,1)S(1)} %bitcast.9, bf16[128,1536]{1,0:T(8,128)(2,1)S(1)} %bitcast.12, bf16[8,1536]{1,0:T(8,128)(2,1)S(1)} %collective-permute-done.1.halo0_ref, ...), custom_call_target="tpu_custom_call" | custom-call | tf_op jit(solution)/shard_map/local/pallas_call | solution.py:160
  34.8 32.4 %all-gather = bf16[3072,128]{1,0:T(8,128)(2,1)S(1)} all-gather(bf16[192,128]{1,0:T(8,128)(2,1)S(1)} %get-tuple-element.8), channel_id=2, replica_groups={{0,32,64,96,128,160,192,224,256,288,320,352,384,416,448,480},{16,48,80,..., dimensions={0}, use_global_device_ids=true | all-gather | bytes 835584 | tf_op jit(solution)/shard_map/all_gather | solution.py:179
  67.2 0.0 copy-done.2
  67.2 2.1 %chain.1.own_ref = f32[192,128]{1,0:T(8,128)S(1)} custom-call(bf16[16,192,128]{2,1,0:T(8,128)(2,1)S(1)} %bitcast.8, bf16[192,128]{1,0:T(8,128)(2,1)S(1)} %get-tuple-element.9.qeff_ref, f32[192,128]{1,0:T(8,128)S(1)} %get-tuple-element.10.oeff_ref, f32[2,3,64,64]{3,2,1,0:T(8,128)S(1)} %copy-done.2), custom_call_target="tpu_custom_call" | custom-call | tf_op jit(solution)/shard_map/chain/pallas_call | solution.py:180
  69.3 10.7 %collective-permute-start.3 = (f32[192,128]{1,0:T(8,128)S(1)}, f32[192,128]{1,0:T(8,128)S(1)}, u32[]{:S(2)}, u32[]{:S(2)}) collective-permute-start(f32[192,128]{1,0:T(8,128)S(1)} %chain.1.own_ref), channel_id=1, source_target_pairs={{0,16},{16,0},{32,48},{48,32},{64,80},{80,64},{96,112},{112,96},{1... | collective-permute-start | bytes 294920 | tf_op jit(solution)/shard_map/ppermute | solution.py:188
  80.0 0.9 collective-permute-done.3.mate_ref
  80.9 0.0 copy-done.1
  80.9 0.5 project.1
  81.5 12.5 %all_to_all.11.parts_ref = bf16[16,8,1536]{2,1,0:T(8,128)(2,1)S(1)} all-to-all(bf16[16,8,1536]{2,1,0:T(8,128)(2,1)S(1)} %bitcast.10), channel_id=1, replica_groups=mesh['seq'=32,'head'=16] {'head'}, dimensions={0} | all-to-all | bytes 786432 | tf_op jit(solution)/shard_map/all_to_all | solution.py:197
  94.0 0.7 total.1
  (5 shorter events, 0.0 us)
Async XLA Ops:
  0.0 67.2 %copy-start.2 = (f32[2,3,64,64]{3,2,1,0:T(8,128)S(1)}, f32[2,3,64,64]{3,2,1,0:T(8,128)}, u32[]{:S(2)}) copy-start(f32[2,3,64,64]{3,2,1,0:T(8,128)} %init_ref.1) | copy-start | bytes 294916
  0.8 80.1 %copy-start.1 = (bf16[192,3072]{1,0:T(8,128)(2,1)S(1)}, bf16[192,3072]{1,0:T(8,128)(2,1)}, u32[]{:S(2)}) copy-start(bf16[192,3072]{1,0:T(8,128)(2,1)} %w_ref.3) | copy-start | bytes 3538948
  16.3 10.5 %collective-permute-start = (bf16[16,8,1536]{2,1,0:T(8,128)(2,1)S(1)}, bf16[16,8,1536]{2,1,0:T(8,128)(2,1)S(1)}, u32[]{:S(2)}, u32[]{:S(2)}) collective-permute-start(bf16[16,8,1536]{2,1,0:T(8,128)(2,1)S(1)} %all_to_all.10), channel_id=1, source_target_pairs={{0,16},{16,0},{32,48},{48,32},{64,80},{80,64},{96,112},{112,96},{1... | collective-permute-start | bytes 1179656 | tf_op jit(solution)/shard_map/ppermute | solution.py:154
  21.5 5.3 %collective-permute-start.2 = (bf16[8,1536]{1,0:T(8,128)(2,1)S(1)}, bf16[8,1536]{1,0:T(8,128)(2,1)S(1)}, u32[]{:S(2)}, u32[]{:S(2)}) collective-permute-start(bf16[8,1536]{1,0:T(8,128)(2,1)S(1)} %slice_bitcast_fusion), channel_id=1, source_target_pairs={{16,48},{48,80},{80,112},{112,144},{144,176},{176,208},{208,240},{... | collective-permute-start | bytes 73736 | tf_op jit(solution)/shard_map/ppermute | solution.py:157
  24.6 2.2 %collective-permute-start.1 = (bf16[8,1536]{1,0:T(8,128)(2,1)S(1)}, bf16[8,1536]{1,0:T(8,128)(2,1)S(1)}, u32[]{:S(2)}, u32[]{:S(2)}) collective-permute-start(bf16[8,1536]{1,0:T(8,128)(2,1)S(1)} %slice_bitcast_fusion), channel_id=1, source_target_pairs={{16,32},{48,64},{80,96},{112,128},{144,160},{176,192},{208,224},{2... | collective-permute-start | bytes 73736 | tf_op jit(solution)/shard_map/ppermute | solution.py:156
  26.8 2.0 %copy-start = (bf16[3,192,3072]{2,1,0:T(8,128)(2,1)S(1)}, bf16[3,192,3072]{2,1,0:T(8,128)(2,1)}, u32[]{:S(2)}) copy-start(bf16[3,192,3072]{2,1,0:T(8,128)(2,1)} %w_ref.2) | copy-start | bytes 10616836
  28.8 0.7 copy-start.3
  29.6 0.7 copy-start.4
  69.3 11.6 %collective-permute-start.3 = (f32[192,128]{1,0:T(8,128)S(1)}, f32[192,128]{1,0:T(8,128)S(1)}, u32[]{:S(2)}, u32[]{:S(2)}) collective-permute-start(f32[192,128]{1,0:T(8,128)S(1)} %chain.1.own_ref), channel_id=1, source_target_pairs={{0,16},{16,0},{32,48},{48,32},{64,80},{80,64},{96,112},{112,96},{1... | collective-permute-start | bytes 294920 | tf_op jit(solution)/shard_map/ppermute | solution.py:188

commit v2 on v1

v2 whole, which is shorter than its diff:
```python
import jax
import jax.numpy as jnp
from jax import lax
from jax.experimental import pallas as pl
from jax.experimental.pallas import tpu as pltpu
from jax.sharding import PartitionSpec as P

MB = 16
KERNEL = 4
EPSILON = 1e-05
F32 = jnp.float32
BF16 = jnp.bfloat16


def mm(a, b, ca=1, cb=0):
    return lax.dot_general(a, b, (((ca,), (cb,)), ((), ())), preferred_element_type=F32)


def cat(parts, axis):
    return jnp.concatenate(parts, axis=axis)


def normed(u):
    centred = u - jnp.mean(u, axis=0, keepdims=True)
    return centred * lax.rsqrt(jnp.mean(centred * centred, axis=0, keepdims=True) + EPSILON)


def role_of(place):
    return (place + place // 2) % 2


def fold_kernel(tokens_ref, lrw_ref, conv_ref, base_ref, out_ref, lrp_ref, taps_ref, rate_ref, wide_ref):
    role = role_of(lax.axis_index("seq"))
    half = out_ref.shape[2]
    for j in range(half // 128):
        cols = slice(j * 128, (j + 1) * 128)
        for part in range(2):
            piece = tokens_ref[:, part * half + j * 128:part * half + (j + 1) * 128].astype(F32)
            wide_ref[j, pl.ds(part, 4, stride=2), :] = piece
        block = wide_ref[j].astype(BF16)
        for i in range(out_ref.shape[0]):
            out_ref[i, :, cols] = block
    lrw = lrw_ref[...].astype(F32)
    whole = jnp.where(role == 0, lrw[0:1], lrw[2:3])
    lrp_ref[...] = cat([whole, lrw[1:2], jnp.zeros((14, lrw.shape[1]), F32)], 0).astype(BF16)
    inner = conv_ref.shape[2]
    taps_rows = cat([conv_ref[0], conv_ref[1]], 0)
    taps_ref[...] = cat([taps_rows, jnp.zeros((2 * KERNEL, 256 - inner), F32)], 1).T
    base = base_ref[...] / MB
    rate_ref[0:1, :] = jnp.broadcast_to(jnp.where(role == 0, base[0:1, 0:1], base[0:1, 2:3]), (1, 128))
    rate_ref[1:2, :] = jnp.broadcast_to(base[0:1, 1:2], (1, 128))


def spread(src_ref, wide_ref, out_ref, row):
    half = src_ref.shape[1]
    for j in range(half // 128):
        wide_ref[j] = src_ref[:, j * 128:(j + 1) * 128].astype(F32)
        for part in range(2):
            cols = slice(part * half + j * 128, part * half + (j + 1) * 128)
            out_ref[pl.ds(row, 64), cols] = wide_ref[j, pl.ds(part, 64, stride=2), :].astype(BF16)


def local_kernel(own_hbm, mate_hbm, halo0_hbm, halo1_hbm, w_hbm, lrp_ref, taps_ref, rate_ref, send_ref, qeff_ref, oeff_ref,
                 own_ref, mate_ref, halo0_ref, halo1_ref, w_ref, wide_ref, tail_ref, xall_ref, sems):
    place = lax.axis_index("seq")
    core = place % 2
    role = role_of(place)
    half = halo0_ref.shape[1]
    fetches = [
        pltpu.make_async_copy(a, b, sems.at[i])
        for i, (a, b) in enumerate(((own_hbm, own_ref), (mate_hbm, mate_ref), (halo0_hbm, halo0_ref), (halo1_hbm, halo1_ref)))
    ]
    used = pl.ds(pl.multiple_of(64 * role, 64), 128)
    pieces = []
    for part in range(2):
        cols = slice(part * half, (part + 1) * half)
        pieces.append(pltpu.make_async_copy(w_hbm.at[:, used, cols], w_ref.at[:, :, cols], sems.at[4 + part]))
    for fetch in fetches + pieces:
        fetch.start()
    fetches[0].wait()
    spread(own_ref, wide_ref, xall_ref, pl.multiple_of(64 * core, 64))
    fetches[1].wait()
    spread(mate_ref, wide_ref, xall_ref, pl.multiple_of(64 * (1 - core), 64))
    fetches[2].wait()
    fetches[3].wait()
    halo = jnp.where(core == 0, halo0_ref[...].astype(F32), halo1_ref[...].astype(F32))
    for j in range(half // 128):
        tail_ref[j, 0:24, :] = jnp.zeros((24, 128), F32)
        tail_ref[j, 24:32, :] = halo[:, j * 128:(j + 1) * 128]
        for part in range(2):
            cols = slice(part * half + j * 128, part * half + (j + 1) * 128)
            xall_ref[240:256, cols] = tail_ref[j, pl.ds(part, 16, stride=2), :].astype(BF16)
    at = pl.multiple_of(128 * role, 64)
    whole = pl.ds(pl.multiple_of(64 * role, 64), 64)
    shared = pl.ds(pl.multiple_of(64 * (1 - role), 64), 64)
    mid = pl.ds(pl.multiple_of(64 - 32 * role, 32), 32)
    proj = None
    for part in range(2):
        cols = slice(part * half, (part + 1) * half)
        pieces[part].wait()
        rows = cat([
            w_ref[0, whole, cols], w_ref[0, shared, cols], w_ref[1, whole, cols], w_ref[1, shared, cols],
            w_ref[2, whole, cols], w_ref[2, mid, cols], lrp_ref[:, cols],
        ], 0)
        term = mm(rows, xall_ref[:, cols], 1, 1)
        proj = term if proj is None else proj + term
    lane = lax.broadcasted_iota(jnp.int32, (128, 128), 1)
    taps = cat([taps_ref[pl.ds(at, 64), :], taps_ref[64:128, :]], 0)
    convs = []
    for i in range(2):
        raw = proj[128 * i:128 * i + 128, 0:128].astype(BF16).astype(F32)
        edge = proj[128 * i:128 * i + 128, 128:256].astype(BF16).astype(F32)
        first = KERNEL * i
        conv = taps[:, first + KERNEL - 1:first + KERNEL] * raw
        for back in range(1, KERNEL):
            moved = jnp.where(lane < back, pltpu.roll(edge, back, 1), pltpu.roll(raw, back, 1))
            conv = conv + taps[:, first + KERNEL - 1 - back:first + KERNEL - back] * moved
        convs.append(conv)

    src = lax.broadcasted_iota(jnp.int32, (128, 128), 0)
    dst = lax.broadcasted_iota(jnp.int32, (128, 128), 1)
    strict = dst // MB > src // MB
    eye = jnp.where(src == dst, 1.0, 0.0).astype(F32)

    maps = []
    for slot in range(2):
        lo, hi = slot * 64, (slot + 1) * 64
        q = convs[0][lo:hi]
        k = convs[1][lo:hi]
        k = k * lax.rsqrt((jnp.mean(k * k, axis=0, keepdims=True) + EPSILON) * 64)
        rate = jax.nn.sigmoid(proj[352 + slot:353 + slot, 0:128]) * rate_ref[slot:slot + 1, :]
        v = proj[256:320, 0:128] if slot == 0 else proj[320:352, 0:128]
        kb = k.astype(BF16)
        kt = kb.T
        grams = mm(kt, cat([kb, q.astype(BF16)], 1))
        u = jnp.where(strict, grams[:, 0:128], 0.0) * rate
        ub = u.astype(BF16)
        u2 = mm(ub, ub)
        u2b = u2.astype(BF16)
        u4 = mm(u2b, u2b)
        t1 = eye - u + u2 - mm(ub, u2b)
        t = t1 + mm(t1.astype(BF16), u4.astype(BF16))
        rev = t.T * rate
        fwd = rev.T
        scores = grams[:, 128:256]
        seen_f = jnp.where(dst >= src, scores, 0.0).astype(BF16)
        seen_r = jnp.where(dst <= src, scores, 0.0).astype(BF16)
        solved_f = mm(fwd.astype(BF16), cat([seen_f, kt], 1)).astype(BF16)
        solved_r = mm(rev.astype(BF16), cat([seen_r, kt], 1)).astype(BF16)
        stacked = cat([kb, v.astype(BF16)], 0)
        pair = []
        for way, solved in enumerate((solved_f, solved_r)):
            both = mm(stacked, solved)
            qeff_ref[way, lo:hi, :] = (q - both[0:64, 0:128]).astype(BF16)
            oeff_ref[way, lo:lo + v.shape[0], :] = both[64:, 0:128]
            pair.append((-both[0:64, 128:192], both[64:, 128:192]))
        maps.append(pair)
    (a0, b0), (a1, b1) = maps[0][0], maps[1][0]
    send_ref[0:64, :] = cat([a0, a1], 1).astype(BF16)
    for way in range(2):
        b0, b1 = maps[0][way][1], maps[1][way][1]
        packed = cat([b0[0:48], cat([b0[48:64], b1], 0)], 1)
        send_ref[64 + 48 * way:112 + 48 * way, :] = packed.astype(BF16)


def chain_kernel(maps_ref, qeff_ref, oeff_ref, init_ref, out_ref):
    place = lax.axis_index("seq")
    role = role_of(place)
    chip = place // 2
    chips = maps_ref.shape[0]
    states = []
    for way in range(2):
        shared = init_ref[way, 1, pl.ds(pl.multiple_of(32 * role, 32), 32), :]
        states.append([init_ref[way, 2 * role], shared])
    for i in range(chips - 1):
        for way in range(2):
            j = i if way == 0 else chips - 1 - i
            live = (j < chip) if way == 0 else (j > chip)
            block = maps_ref[j]
            whole, shared = states[way]
            at = 64 + 48 * way
            b0 = cat([block[at:at + 48, 0:64], block[at:at + 16, 64:128]], 0).astype(F32)
            b1 = block[at + 16:at + 48, 64:128].astype(F32)
            new0 = whole + mm(whole.astype(BF16), block[0:64, 0:64], 1, way) + b0
            new1 = shared + mm(shared.astype(BF16), block[0:64, 64:128], 1, way) + b1
            states[way] = [jnp.where(live, new0, whole), jnp.where(live, new1, shared)]
    sums = None
    for way in range(2):
        whole = mm(states[way][0].astype(BF16), qeff_ref[way, 0:64, :]) + oeff_ref[way, 0:64, :]
        sums = normed(whole) if sums is None else sums + normed(whole)
        shared = mm(states[way][1].astype(BF16), qeff_ref[way, 64:128, :]) + oeff_ref[way, 64:96, :]
        out_ref[64 + 32 * way:96 + 32 * way, :] = shared
    out_ref[0:64, :] = sums


def output_kernel(mine_ref, mate_ref, w_ref, out_ref):
    place = lax.axis_index("seq")
    core = place % 2
    role = role_of(place)
    mine = mine_ref[...]
    mate = mate_ref[...]
    low = jnp.where(role == 0, mine, mate)
    high = jnp.where(role == 0, mate, mine)
    middle = normed(cat([low[64:96], high[64:96]], 0)) + normed(cat([low[96:128], high[96:128]], 0))
    hidden = cat([low[0:64], middle, high[0:64]], 0).astype(BF16)
    row = lax.broadcasted_iota(jnp.int32, (128, 128), 0)
    col = lax.broadcasted_iota(jnp.int32, (128, 128), 1)
    pick = jnp.where(col == row // 2 + 64 * core, 1.0, 0.0).astype(BF16)
    twice = mm(pick, hidden, 1, 1).astype(BF16)
    half = out_ref.shape[1]
    even = lax.broadcasted_iota(jnp.int32, (128, half), 0) % 2 == 0
    first = mm(twice, w_ref[:, 0:half])
    second = mm(twice, w_ref[:, half:2 * half])
    out_ref[...] = jnp.where(even, first, second).astype(BF16)


def total_kernel(parts_ref, out_ref, wide_ref):
    acc = parts_ref[0].astype(F32)
    for i in range(1, parts_ref.shape[0]):
        acc = acc + parts_ref[i].astype(F32)
    half = acc.shape[1]
    for j in range(half // 128):
        wide_ref[j] = acc[:, j * 128:(j + 1) * 128]
        for part in range(2):
            out_ref[:, part * half + j * 128:part * half + (j + 1) * 128] = (
                wide_ref[j, pl.ds(part, 4, stride=2), :].astype(BF16))


def shards(tokens, w_qkv, lr_weight, lr_base, conv_weight, w_init, w_out):
    width = tokens.shape[1]
    half = width // 2
    inner = w_qkv.shape[1]
    n_seq = lax.axis_size("seq")
    n_head = lax.axis_size("head")
    params = pltpu.CompilerParams(vmem_limit_bytes=24 * 1024 * 1024)
    vmem = pl.BlockSpec(memory_space=pltpu.VMEM)
    hbm = pl.BlockSpec(memory_space=pl.ANY)

    folded, lr_rows, taps, base = pl.pallas_call(
        fold_kernel,
        out_shape=(
            jax.ShapeDtypeStruct((n_head, 8, half), BF16),
            jax.ShapeDtypeStruct((16, width), BF16),
            jax.ShapeDtypeStruct((256, 2 * KERNEL), F32),
            jax.ShapeDtypeStruct((8, 128), F32),
        ),
        in_specs=[vmem] * 4,
        out_specs=(vmem,) * 4,
        scratch_shapes=[pltpu.VMEM((half // 128, 8, 128), F32)],
        compiler_params=params,
        name="fold",
    )(tokens, lr_weight, conv_weight, lr_base.reshape(1, lr_base.shape[0]))
    own = lax.all_to_all(folded, "head", 0, 0)
    swap = [(i, i ^ 1) for i in range(n_seq)]
    mate = lax.ppermute(own, "seq", swap)
    tail = own[n_head - 1]
    halo0 = lax.ppermute(tail, "seq", [(i, i + 1) for i in range(1, n_seq - 1, 2)])
    halo1 = lax.ppermute(tail, "seq", [(i, i + 2) for i in range(1, n_seq - 2, 2)])
    send, qeff, oeff = pl.pallas_call(
        local_kernel,
        out_shape=(
            jax.ShapeDtypeStruct((160, 128), BF16),
            jax.ShapeDtypeStruct((2, 128, 128), BF16),
            jax.ShapeDtypeStruct((2, 96, 128), F32),
        ),
        in_specs=[hbm] * 5 + [vmem] * 3,
        out_specs=(vmem, vmem, vmem),
        scratch_shapes=[
            pltpu.VMEM((n_head * 8, half), BF16),
            pltpu.VMEM((n_head * 8, half), BF16),
            pltpu.VMEM((8, half), BF16),
            pltpu.VMEM((8, half), BF16),
            pltpu.VMEM((3, 128, width), BF16),
            pltpu.VMEM((half // 128, 128, 128), F32),
            pltpu.VMEM((half // 128, 32, 128), F32),
            pltpu.VMEM((256, width), BF16),
            pltpu.SemaphoreType.DMA((6,)),
        ],
        compiler_params=pltpu.CompilerParams(vmem_limit_bytes=51 * 1024 * 1024),
        name="local",
    )(own.reshape(n_head * 8, half), mate.reshape(n_head * 8, half), halo0, halo1, w_qkv, lr_rows, taps, base)

    groups = [[2 * j + (c + j) % 2 for j in range(n_seq // 2)] for c in range(2)]
    received = lax.all_gather(send, "seq", axis_index_groups=groups)
    rows = pl.pallas_call(
        chain_kernel,
        out_shape=jax.ShapeDtypeStruct((128, 128), F32),
        in_specs=[vmem] * 4,
        out_specs=vmem,
        compiler_params=params,
        name="chain",
    )(received, qeff, oeff, w_init)
    other = lax.ppermute(rows, "seq", swap)
    partial = pl.pallas_call(
        output_kernel,
        out_shape=jax.ShapeDtypeStruct((n_head * 8, half), BF16),
        in_specs=[vmem] * 3,
        out_specs=vmem,
        compiler_params=params,
        name="output",
    )(rows, other, w_out)
    parts = lax.all_to_all(partial.reshape(n_head, 8, half), "head", 0, 0)
    return pl.pallas_call(
        total_kernel,
        out_shape=jax.ShapeDtypeStruct(tokens.shape, BF16),
        in_specs=[vmem],
        out_specs=vmem,
        scratch_shapes=[pltpu.VMEM((half // 128, 8, 128), F32)],
        compiler_params=params,
        name="total",
    )(parts)


def solution(mesh):
    placed = (
        P(("seq", "head"), None),
        P(None, "head", None),
        P("head", None),
        P("head"),
        P(None, None, "head"),
        P(None, "head", None, None),
        P("head", None),
    )
    return jax.shard_map(
        shards, mesh=mesh, in_specs=placed, out_specs=P(("seq", "head"), None), check_vma=False
    )
```

time: 95 us -> 89.8 us (0.945)
  starting transfers between devices: 20.2 us -> 11.5 us
  blocking collectives: 60.4 us -> 64.2 us
  local copies, waits for them, and re-layouts: 5.05 us -> 2.88 us
  waiting for transfers between devices: 1.01 us -> 2.12 us
    ppermute x1, starting transfers between devices: 10.7 us -> 1.95 us  [shards(): other = lax.ppermute(rows, 'seq', swap)]
    all_gather x1, blocking collectives: 32.4 us -> 36.2 us  [shards(): received = lax.all_gather(send, 'seq', axis_index_groups=groups)]
    pallas_call x3 -> x4, Pallas kernels: 7.19 us -> 7.94 us  [the longest x1 5.21 us: shards(): pl.pallas_call(local_kernel, out_shape=(jax.ShapeDtypeStruct((160, 128),...]
    unnamed x10 -> x12, local copies, waits for them, and re-layouts: 3.4 us -> 2.87 us
  transfers between devices with their start and end apart: 4 -> 4, of which waited for: 2 -> 2; matrix products, arithmetic and copies ran while one was open for 1% -> 0% of each run, Pallas kernels for 0% -> 0%
where the time goes in v2:
time: 89.8 us; the launch traced here: 89.4 us
  blocking collectives  64.2 us (71%)
  starting transfers between devices  11.5 us (13%)
  Pallas kernels  8.62 us (10%)
  local copies, waits for them, and re-layouts  2.88 us (3%)
  waiting for transfers between devices  2.12 us (2%)
    all_gather x1, blocking collectives, shards(): received = lax.all_gather(send, 'seq', axis_index_groups=groups)  36.2 us
    all_to_all x1, blocking collectives, shards(): own = lax.all_to_all(folded, 'head', 0, 0)  15.5 us
    all_to_all x1, blocking collectives, shards(): parts = lax.all_to_all(partial.reshape(n_head, 8, half), 'head', 0, 0)  12.5 us
    pallas_call x1, Pallas kernels, shards(): pl.pallas_call(local_kernel, out_shape=(jax.ShapeDtypeStruct((160, 128),...  5.21 us
    ppermute x1, starting transfers between devices, shards(): mate = lax.ppermute(own, 'seq', swap)  5.13 us
    ppermute x1, starting transfers between devices, shards(): lax.ppermute(tail, 'seq', [(i, i + 2) for i in range(1, n_seq - 2, 2)])  3.11 us
    unnamed x12, local copies, waits for them, and re-layouts  2.87 us
    pallas_call x1, Pallas kernels, shards(): pl.pallas_call(chain_kernel, out_shape=jax.ShapeDtypeStruct((128, 128), F...  1.99 us
  transfers between devices with their start and end apart: 4, of which 2 were waited for; matrix products, arithmetic and copies ran while one was open for 0% of the time, Pallas kernels for 0%

profile of v2, /device:TPU:1, one launch (start us, length us, event | category | flops | bytes accessed | tf_op | source)
XLA Modules:
  0.0 89.4 jit_solution(11253263507130500118)
XLA Ops:
  0.0 0.0 copy-start.1
  0.0 0.0 copy-start.2
  0.0 0.8 copy-done.2
  0.8 0.7 copy-done.3
  1.5 0.7 copy-done.4
  2.2 0.7 copy-done.5
  2.9 0.2 fold.1
  3.0 15.5 %all_to_all.10 = bf16[16,8,1536]{2,1,0:T(8,128)(2,1)S(1)} all-to-all(bf16[16,8,1536]{2,1,0:T(8,128)(2,1)S(1)} %get-tuple-element.12), channel_id=1, replica_groups=mesh['seq'=32,'head'=16] {'head'}, dimensions={0} | all-to-all | bytes 786432 | tf_op jit(solution)/shard_map/all_to_all | solution.py:253
  18.5 5.1 %collective-permute-start = (bf16[16,8,1536]{2,1,0:T(8,128)(2,1)S(1)}, bf16[16,8,1536]{2,1,0:T(8,128)(2,1)S(1)}, u32[]{:S(2)}, u32[]{:S(2)}) collective-permute-start(bf16[16,8,1536]{2,1,0:T(8,128)(2,1)S(1)} %all_to_all.10), channel_id=1, source_target_pairs={{0,16},{16,0},{32,48},{48,32},{64,80},{80,64},{96,112},{112,96},{1... | collective-permute-start | bytes 1179656 | tf_op jit(solution)/shard_map/ppermute | solution.py:255
  23.7 3.1 %collective-permute-start.2 = (bf16[8,1536]{1,0:T(8,128)(2,1)S(1)}, bf16[8,1536]{1,0:T(8,128)(2,1)S(1)}, u32[]{:S(2)}, u32[]{:S(2)}) collective-permute-start(bf16[8,1536]{1,0:T(8,128)(2,1)S(1)} %slice_bitcast_fusion), channel_id=1, source_target_pairs={{16,48},{48,80},{80,112},{112,144},{144,176},{176,208},{208,240},{... | collective-permute-start | bytes 73736 | tf_op jit(solution)/shard_map/ppermute | solution.py:258
  26.8 1.3 %collective-permute-start.1 = (bf16[8,1536]{1,0:T(8,128)(2,1)S(1)}, bf16[8,1536]{1,0:T(8,128)(2,1)S(1)}, u32[]{:S(2)}, u32[]{:S(2)}) collective-permute-start(bf16[8,1536]{1,0:T(8,128)(2,1)S(1)} %slice_bitcast_fusion), channel_id=1, source_target_pairs={{16,32},{48,64},{80,96},{112,128},{144,160},{176,192},{208,224},{2... | collective-permute-start | bytes 73736 | tf_op jit(solution)/shard_map/ppermute | solution.py:257
  28.1 0.0 collective-permute-done.2.halo1_hbm
  28.1 0.9 %collective-permute-done.1.halo0_hbm = bf16[8,1536]{1,0:T(8,128)(2,1)S(1)} collective-permute-done((bf16[8,1536]{1,0:T(8,128)(2,1)S(1)}, bf16[8,1536]{1,0:T(8,128)(2,1)S(1)}, u32[]{:S(2)}, u32[]{:S(2)}) %collective-permute-start.1) | collective-permute-done | bytes 24608 | tf_op jit(solution)/shard_map/ppermute | solution.py:257
  29.0 0.0 collective-permute-done
  29.0 5.2 %local.1 = (bf16[160,128]{1,0:T(8,128)(2,1)S(1)}, bf16[2,128,128]{2,1,0:T(8,128)(2,1)S(1)}, f32[2,96,128]{2,1,0:T(8,128)S(1)}) custom-call(bf16[128,1536]{1,0:T(8,128)(2,1)S(1)} %bitcast.8, bf16[128,1536]{1,0:T(8,128)(2,1)S(1)} %bitcast.10, bf16[8,1536]{1,0:T(8,128)(2,1)S(1)} %collective-permute-done.1.halo0_hbm, ...), custom_call_target="tpu_custom_call" | custom-call | tf_op jit(solution)/shard_map/local/pallas_call | solution.py:259
  34.2 36.2 %all-gather = bf16[2560,128]{1,0:T(8,128)(2,1)S(1)} all-gather(bf16[160,128]{1,0:T(8,128)(2,1)S(1)} %get-tuple-element.16), channel_id=2, replica_groups={{0,48,64,112,128,176,192,240,256,304,320,368,384,432,448,496},{16,32,80..., dimensions={0}, use_global_device_ids=true | all-gather | bytes 696320 | tf_op jit(solution)/shard_map/all_gather | solution.py:284
  70.4 0.0 copy-done.1
  70.4 2.0 %chain.1.mine_ref = f32[128,128]{1,0:T(8,128)S(1)} custom-call(bf16[16,160,128]{2,1,0:T(8,128)(2,1)S(1)} %bitcast.7, bf16[2,128,128]{2,1,0:T(8,128)(2,1)S(1)} %get-tuple-element.17.qeff_ref, f32[2,96,128]{2,1,0:T(8,128)S(1)} %get-tuple-element.18.oeff_ref, f32[2,3,64,64]{3,2,1,0:T(8,128)S(1)} %copy-done.1), custom_call_target="tpu_custom_call" | custom-call | tf_op jit(solution)/shard_map/chain/pallas_call | solution.py:285
  72.4 1.9 %collective-permute-start.3 = (f32[128,128]{1,0:T(8,128)S(1)}, f32[128,128]{1,0:T(8,128)S(1)}, u32[]{:S(2)}, u32[]{:S(2)}) collective-permute-start(f32[128,128]{1,0:T(8,128)S(1)} %chain.1.mine_ref), channel_id=1, source_target_pairs={{0,16},{16,0},{32,48},{48,32},{64,80},{80,64},{96,112},{112,96},{1... | collective-permute-start | bytes 196616 | tf_op jit(solution)/shard_map/ppermute | solution.py:293
  74.4 1.2 %collective-permute-done.3.mate_ref = f32[128,128]{1,0:T(8,128)S(1)} collective-permute-done((f32[128,128]{1,0:T(8,128)S(1)}, f32[128,128]{1,0:T(8,128)S(1)}, u32[]{:S(2)}, u32[]{:S(2)}) %collective-permute-start.3) | collective-permute-done | bytes 65568 | tf_op jit(solution)/shard_map/ppermute | solution.py:293
  75.6 0.0 copy-done
  75.6 0.6 output.1
  76.1 12.5 %all_to_all.11.parts_ref = bf16[16,8,1536]{2,1,0:T(8,128)(2,1)S(1)} all-to-all(bf16[16,8,1536]{2,1,0:T(8,128)(2,1)S(1)} %bitcast.9), channel_id=1, replica_groups=mesh['seq'=32,'head'=16] {'head'}, dimensions={0} | all-to-all | bytes 786432 | tf_op jit(solution)/shard_map/all_to_all | solution.py:302
  88.7 0.7 total.1
  (5 shorter events, 0.0 us)
Async XLA Ops:
  0.0 70.4 %copy-start.1 = (f32[2,3,64,64]{3,2,1,0:T(8,128)S(1)}, f32[2,3,64,64]{3,2,1,0:T(8,128)}, u32[]{:S(2)}) copy-start(f32[2,3,64,64]{3,2,1,0:T(8,128)} %init_ref.1) | copy-start | bytes 294916
  0.0 0.8 copy-start.2
  0.8 0.7 copy-start.3
  1.5 0.7 copy-start.4
  2.2 0.7 copy-start.5
  3.0 72.5 %copy-start = (bf16[192,3072]{1,0:T(8,128)(2,1)S(1)}, bf16[192,3072]{1,0:T(8,128)(2,1)}, u32[]{:S(2)}) copy-start(bf16[192,3072]{1,0:T(8,128)(2,1)} %w_ref.1) | copy-start | bytes 3538948
  18.5 10.5 %collective-permute-start = (bf16[16,8,1536]{2,1,0:T(8,128)(2,1)S(1)}, bf16[16,8,1536]{2,1,0:T(8,128)(2,1)S(1)}, u32[]{:S(2)}, u32[]{:S(2)}) collective-permute-start(bf16[16,8,1536]{2,1,0:T(8,128)(2,1)S(1)} %all_to_all.10), channel_id=1, source_target_pairs={{0,16},{16,0},{32,48},{48,32},{64,80},{80,64},{96,112},{112,96},{1... | collective-permute-start | bytes 1179656 | tf_op jit(solution)/shard_map/ppermute | solution.py:255
  23.7 4.4 %collective-permute-start.2 = (bf16[8,1536]{1,0:T(8,128)(2,1)S(1)}, bf16[8,1536]{1,0:T(8,128)(2,1)S(1)}, u32[]{:S(2)}, u32[]{:S(2)}) collective-permute-start(bf16[8,1536]{1,0:T(8,128)(2,1)S(1)} %slice_bitcast_fusion), channel_id=1, source_target_pairs={{16,48},{48,80},{80,112},{112,144},{144,176},{176,208},{208,240},{... | collective-permute-start | bytes 73736 | tf_op jit(solution)/shard_map/ppermute | solution.py:258
  26.8 2.2 %collective-permute-start.1 = (bf16[8,1536]{1,0:T(8,128)(2,1)S(1)}, bf16[8,1536]{1,0:T(8,128)(2,1)S(1)}, u32[]{:S(2)}, u32[]{:S(2)}) collective-permute-start(bf16[8,1536]{1,0:T(8,128)(2,1)S(1)} %slice_bitcast_fusion), channel_id=1, source_target_pairs={{16,32},{48,64},{80,96},{112,128},{144,160},{176,192},{208,224},{2... | collective-permute-start | bytes 73736 | tf_op jit(solution)/shard_map/ppermute | solution.py:257
  72.4 3.1 %collective-permute-start.3 = (f32[128,128]{1,0:T(8,128)S(1)}, f32[128,128]{1,0:T(8,128)S(1)}, u32[]{:S(2)}, u32[]{:S(2)}) collective-permute-start(f32[128,128]{1,0:T(8,128)S(1)} %chain.1.mine_ref), channel_id=1, source_target_pairs={{0,16},{16,0},{32,48},{48,32},{64,80},{80,64},{96,112},{112,96},{1... | collective-permute-start | bytes 196616 | tf_op jit(solution)/shard_map/ppermute | solution.py:293

commit v3 on v2

--- a/solution.py
+++ b/solution.py
@@ -29,8 +29,7 @@
     return (place + place // 2) % 2
 
 
-def fold_kernel(tokens_ref, lrw_ref, conv_ref, base_ref, out_ref, lrp_ref, taps_ref, rate_ref, wide_ref):
-    role = role_of(lax.axis_index("seq"))
+def fold_kernel(tokens_ref, out_ref, wide_ref):
     half = out_ref.shape[2]
     for j in range(half // 128):
         cols = slice(j * 128, (j + 1) * 128)
@@ -40,6 +39,13 @@
         block = wide_ref[j].astype(BF16)
         for i in range(out_ref.shape[0]):
             out_ref[i, :, cols] = block
+
+
+def prepare_kernel(w_hbm, lrw_ref, conv_ref, base_ref, w_ref, lrp_ref, taps_ref, rate_ref, sem):
+    role = role_of(lax.axis_index("seq"))
+    used = pl.ds(pl.multiple_of(64 * role, 64), 128)
+    fetch = pltpu.make_async_copy(w_hbm.at[:, used, :], w_ref, sem)
+    fetch.start()
     lrw = lrw_ref[...].astype(F32)
     whole = jnp.where(role == 0, lrw[0:1], lrw[2:3])
     lrp_ref[...] = cat([whole, lrw[1:2], jnp.zeros((14, lrw.shape[1]), F32)], 0).astype(BF16)
@@ -47,8 +53,10 @@
     taps_rows = cat([conv_ref[0], conv_ref[1]], 0)
     taps_ref[...] = cat([taps_rows, jnp.zeros((2 * KERNEL, 256 - inner), F32)], 1).T
     base = base_ref[...] / MB
+    rate_ref[...] = jnp.zeros_like(rate_ref)
     rate_ref[0:1, :] = jnp.broadcast_to(jnp.where(role == 0, base[0:1, 0:1], base[0:1, 2:3]), (1, 128))
     rate_ref[1:2, :] = jnp.broadcast_to(base[0:1, 1:2], (1, 128))
+    fetch.wait()
 
 
 def spread(src_ref, wide_ref, out_ref, row):
@@ -60,29 +68,14 @@
             out_ref[pl.ds(row, 64), cols] = wide_ref[j, pl.ds(part, 64, stride=2), :].astype(BF16)
 
 
-def local_kernel(own_hbm, mate_hbm, halo0_hbm, halo1_hbm, w_hbm, lrp_ref, taps_ref, rate_ref, send_ref, qeff_ref, oeff_ref,
-                 own_ref, mate_ref, halo0_ref, halo1_ref, w_ref, wide_ref, tail_ref, xall_ref, sems):
+def local_kernel(own_ref, mate_ref, halo0_ref, halo1_ref, w_ref, lrp_ref, taps_ref, rate_ref,
+                 send_ref, qeff_ref, oeff_ref, wide_ref, tail_ref, xall_ref):
     place = lax.axis_index("seq")
     core = place % 2
     role = role_of(place)
     half = halo0_ref.shape[1]
-    fetches = [
-        pltpu.make_async_copy(a, b, sems.at[i])
-        for i, (a, b) in enumerate(((own_hbm, own_ref), (mate_hbm, mate_ref), (halo0_hbm, halo0_ref), (halo1_hbm, halo1_ref)))
-    ]
-    used = pl.ds(pl.multiple_of(64 * role, 64), 128)
-    pieces = []
-    for part in range(2):
-        cols = slice(part * half, (part + 1) * half)
-        pieces.append(pltpu.make_async_copy(w_hbm.at[:, used, cols], w_ref.at[:, :, cols], sems.at[4 + part]))
-    for fetch in fetches + pieces:
-        fetch.start()
-    fetches[0].wait()
     spread(own_ref, wide_ref, xall_ref, pl.multiple_of(64 * core, 64))
-    fetches[1].wait()
     spread(mate_ref, wide_ref, xall_ref, pl.multiple_of(64 * (1 - core), 64))
-    fetches[2].wait()
-    fetches[3].wait()
     halo = jnp.where(core == 0, halo0_ref[...].astype(F32), halo1_ref[...].astype(F32))
     for j in range(half // 128):
         tail_ref[j, 0:24, :] = jnp.zeros((24, 128), F32)
@@ -94,16 +87,11 @@
     whole = pl.ds(pl.multiple_of(64 * role, 64), 64)
     shared = pl.ds(pl.multiple_of(64 * (1 - role), 64), 64)
     mid = pl.ds(pl.multiple_of(64 - 32 * role, 32), 32)
-    proj = None
-    for part in range(2):
-        cols = slice(part * half, (part + 1) * half)
-        pieces[part].wait()
-        rows = cat([
-            w_ref[0, whole, cols], w_ref[0, shared, cols], w_ref[1, whole, cols], w_ref[1, shared, cols],
-            w_ref[2, whole, cols], w_ref[2, mid, cols], lrp_ref[:, cols],
-        ], 0)
-        term = mm(rows, xall_ref[:, cols], 1, 1)
-        proj = term if proj is None else proj + term
+    rows = cat([
+        w_ref[0, whole, :], w_ref[0, shared, :], w_ref[1, whole, :], w_ref[1, shared, :],
+        w_ref[2, whole, :], w_ref[2, mid, :], lrp_ref[...],
+    ], 0)
+    proj = mm(rows, xall_ref[...], 1, 1)
     lane = lax.broadcasted_iota(jnp.int32, (128, 128), 1)
     taps = cat([taps_ref[pl.ds(at, 64), :], taps_ref[64:128, :]], 0)
     convs = []
@@ -236,21 +224,31 @@
     vmem = pl.BlockSpec(memory_space=pltpu.VMEM)
     hbm = pl.BlockSpec(memory_space=pl.ANY)
 
-    folded, lr_rows, taps, base = pl.pallas_call(
+    folded = pl.pallas_call(
         fold_kernel,
+        out_shape=jax.ShapeDtypeStruct((n_head, 8, half), BF16),
+        in_specs=[vmem],
+        out_specs=vmem,
+        scratch_shapes=[pltpu.VMEM((half // 128, 8, 128), F32)],
+        compiler_params=params,
+        name="fold",
+    )(tokens)
+    own = lax.all_to_all(folded, "head", 0, 0)
+    weights, lr_rows, taps, base = pl.pallas_call(
+        prepare_kernel,
         out_shape=(
-            jax.ShapeDtypeStruct((n_head, 8, half), BF16),
+            jax.ShapeDtypeStruct((3, 128, width), BF16),
             jax.ShapeDtypeStruct((16, width), BF16),
             jax.ShapeDtypeStruct((256, 2 * KERNEL), F32),
             jax.ShapeDtypeStruct((8, 128), F32),
         ),
-        in_specs=[vmem] * 4,
+        in_specs=[hbm] + [vmem] * 3,
         out_specs=(vmem,) * 4,
-        scratch_shapes=[pltpu.VMEM((half // 128, 8, 128), F32)],
-        compiler_params=params,
-        name="fold",
-    )(tokens, lr_weight, conv_weight, lr_base.reshape(1, lr_base.shape[0]))
-    own = lax.all_to_all(folded, "head", 0, 0)
+        scratch_shapes=[pltpu.SemaphoreType.DMA(())],
+        compiler_params=params,
+        name="prepare",
+    )(w_qkv, lr_weight, conv_weight, lr_base.reshape(1, lr_base.shape[0]))
+    own, weights = lax.optimization_barrier((own, weights))
     swap = [(i, i ^ 1) for i in range(n_seq)]
     mate = lax.ppermute(own, "seq", swap)
     tail = own[n_head - 1]
@@ -263,22 +261,16 @@
             jax.ShapeDtypeStruct((2, 128, 128), BF16),
             jax.ShapeDtypeStruct((2, 96, 128), F32),
         ),
-        in_specs=[hbm] * 5 + [vmem] * 3,
+        in_specs=[vmem] * 8,
         out_specs=(vmem, vmem, vmem),
         scratch_shapes=[
-            pltpu.VMEM((n_head * 8, half), BF16),
-            pltpu.VMEM((n_head * 8, half), BF16),
-            pltpu.VMEM((8, half), BF16),
-            pltpu.VMEM((8, half), BF16),
-            pltpu.VMEM((3, 128, width), BF16),
             pltpu.VMEM((half // 128, 128, 128), F32),
             pltpu.VMEM((half // 128, 32, 128), F32),
             pltpu.VMEM((256, width), BF16),
-            pltpu.SemaphoreType.DMA((6,)),
         ],
-        compiler_params=pltpu.CompilerParams(vmem_limit_bytes=51 * 1024 * 1024),
+        compiler_params=params,
         name="local",
-    )(own.reshape(n_head * 8, half), mate.reshape(n_head * 8, half), halo0, halo1, w_qkv, lr_rows, taps, base)
+    )(own.reshape(n_head * 8, half), mate.reshape(n_head * 8, half), halo0, halo1, weights, lr_rows, taps, base)
 
     groups = [[2 * j + (c + j) % 2 for j in range(n_seq // 2)] for c in range(2)]
     received = lax.all_gather(send, "seq", axis_index_groups=groups)

time: 89.8 us -> 86.5 us (0.963)
  blocking collectives: 64.2 us -> 48.7 us
  starting transfers between devices: 11.5 us -> 19 us
  waiting for transfers between devices: 2.12 us -> 5.7 us
  local copies, waits for them, and re-layouts: 2.88 us -> 4.83 us
  Pallas kernels: 8.62 us -> 7.63 us
    all_to_all x1 -> x0, blocking collectives: 15.5 us -> none  [shards(): own = lax.all_to_all(folded, 'head', 0, 0)]
    all_to_all x0 -> x1, starting transfers between devices: none -> 7.58 us  [shards(): own = lax.all_to_all(folded, 'head', 0, 0)]
    all_to_all x0 -> x1, waiting for transfers between devices: none -> 3.58 us  [shards(): own = lax.all_to_all(folded, 'head', 0, 0)]
    unnamed x12 -> x14, local copies, waits for them, and re-layouts: 2.87 us -> 4.83 us
    pallas_call x1, Pallas kernels: 5.21 us -> 3.28 us  [shards(): pl.pallas_call(local_kernel, out_shape=(jax.ShapeDtypeStruct((160, 128),...]
    pallas_call x1 -> x2, Pallas kernels: 0.17 us -> 1.11 us  [the longest x1 0.81 us: shards(): pl.pallas_call(fold_kernel, out_shape=jax.ShapeDtypeStruct((n_head, 8, ha...]
  transfers between devices with their start and end apart: 4 -> 5, of which waited for: 2 -> 3; matrix products, arithmetic and copies ran while one was open for 0% -> 0% of each run, Pallas kernels for 0% -> 0%
where the time goes in v3:
time: 86.5 us; the launch traced here: 86 us
  blocking collectives  48.7 us (56%)
  starting transfers between devices  19 us (22%)
  Pallas kernels  7.63 us (9%)
  waiting for transfers between devices  5.7 us (7%)
  local copies, waits for them, and re-layouts  4.83 us (6%)
    all_gather x1, blocking collectives, shards(): received = lax.all_gather(send, 'seq', axis_index_groups=groups)  36.2 us
    all_to_all x1, blocking collectives, shards(): parts = lax.all_to_all(partial.reshape(n_head, 8, half), 'head', 0, 0)  12.5 us
    all_to_all x1, starting transfers between devices, shards(): own = lax.all_to_all(folded, 'head', 0, 0)  7.58 us
    ppermute x1, starting transfers between devices, shards(): mate = lax.ppermute(own, 'seq', swap)  5.81 us
    unnamed x14, local copies, waits for them, and re-layouts  4.83 us
    all_to_all x1, waiting for transfers between devices, shards(): own = lax.all_to_all(folded, 'head', 0, 0)  3.58 us
    pallas_call x1, Pallas kernels, shards(): pl.pallas_call(local_kernel, out_shape=(jax.ShapeDtypeStruct((160, 128),...  3.28 us
    ppermute x1, starting transfers between devices, shards(): lax.ppermute(tail, 'seq', [(i, i + 2) for i in range(1, n_seq - 2, 2)])  2.4 us
  transfers between devices with their start and end apart: 5, of which 3 were waited for; matrix products, arithmetic and copies ran while one was open for 0% of the time, Pallas kernels for 0%

profile of v3, /device:TPU:1, one launch (start us, length us, event | category | flops | bytes accessed | tf_op | source)
XLA Modules:
  0.0 86.0 jit_solution(9131807839718547283)
XLA Ops:
  0.0 0.7 copy-done.4
  0.7 0.8 fold.1
  1.5 7.6 %all-to-all-start = ((bf16[16,8,1536]{2,1,0:T(8,128)(2,1)}), bf16[16,8,1536]{2,1,0:T(8,128)(2,1)S(1)}, u32[]{:S(2)}, u32[]{:S(2)}) async-start(bf16[16,8,1536]{2,1,0:T(8,128)(2,1)} %fold.1), calls=%async_computation | async-start | bytes 786432 | tf_op jit(solution)/shard_map/all_to_all | solution.py:236
  9.1 0.0 copy-start
  9.1 2.0 %copy-done = bf16[3,192,3072]{2,1,0:T(8,128)(2,1)S(1)} copy-done((bf16[3,192,3072]{2,1,0:T(8,128)(2,1)S(1)}, bf16[3,192,3072]{2,1,0:T(8,128)(2,1)}, u32[]{:S(2)}) %copy-start) | copy-done | bytes 3538968
  11.1 0.7 copy-done.3
  11.9 0.7 copy-done.5
  12.6 0.7 copy-done.6
  13.2 0.3 prepare.1
  13.5 0.0 copy-start.2
  13.6 3.6 %all-to-all-done = bf16[16,8,1536]{2,1,0:T(8,128)(2,1)S(1)} async-done(((bf16[16,8,1536]{2,1,0:T(8,128)(2,1)}), bf16[16,8,1536]{2,1,0:T(8,128)(2,1)S(1)}, u32[]{:S(2)}, u32[]{:S(2)}) %all-to-all-start) | async-done | bytes 393248 | tf_op jit(solution)/shard_map/all_to_all | solution.py:236
  17.1 5.8 %collective-permute-start = (bf16[16,8,1536]{2,1,0:T(8,128)(2,1)S(1)}, bf16[16,8,1536]{2,1,0:T(8,128)(2,1)S(1)}, u32[]{:S(2)}, u32[]{:S(2)}) collective-permute-start(bf16[16,8,1536]{2,1,0:T(8,128)(2,1)S(1)} %all-to-all-done), channel_id=1, source_target_pairs={{0,16},{16,0},{32,48},{48,32},{64,80},{80,64},{96,112},{112,96},{1... | collective-permute-start | bytes 1179656 | tf_op jit(solution)/shard_map/ppermute | solution.py:253
  23.0 2.4 %collective-permute-start.2 = (bf16[8,1536]{1,0:T(8,128)(2,1)S(1)}, bf16[8,1536]{1,0:T(8,128)(2,1)S(1)}, u32[]{:S(2)}, u32[]{:S(2)}) collective-permute-start(bf16[8,1536]{1,0:T(8,128)(2,1)S(1)} %slice_bitcast_fusion), channel_id=1, source_target_pairs={{16,48},{48,80},{80,112},{112,144},{144,176},{176,208},{208,240},{... | collective-permute-start | bytes 73736 | tf_op jit(solution)/shard_map/ppermute | solution.py:256
  25.4 1.3 %collective-permute-start.1 = (bf16[8,1536]{1,0:T(8,128)(2,1)S(1)}, bf16[8,1536]{1,0:T(8,128)(2,1)S(1)}, u32[]{:S(2)}, u32[]{:S(2)}) collective-permute-start(bf16[8,1536]{1,0:T(8,128)(2,1)S(1)} %slice_bitcast_fusion), channel_id=1, source_target_pairs={{16,32},{48,64},{80,96},{112,128},{144,160},{176,192},{208,224},{2... | collective-permute-start | bytes 73736 | tf_op jit(solution)/shard_map/ppermute | solution.py:255
  26.7 0.0 collective-permute-done.2.halo1_ref
  26.7 0.9 %collective-permute-done.1.halo0_ref = bf16[8,1536]{1,0:T(8,128)(2,1)S(1)} collective-permute-done((bf16[8,1536]{1,0:T(8,128)(2,1)S(1)}, bf16[8,1536]{1,0:T(8,128)(2,1)S(1)}, u32[]{:S(2)}, u32[]{:S(2)}) %collective-permute-start.1) | collective-permute-done | bytes 24608 | tf_op jit(solution)/shard_map/ppermute | solution.py:255
  27.6 3.3 %local.1 = (bf16[160,128]{1,0:T(8,128)(2,1)S(1)}, bf16[2,128,128]{2,1,0:T(8,128)(2,1)S(1)}, f32[2,96,128]{2,1,0:T(8,128)S(1)}) custom-call(bf16[128,1536]{1,0:T(8,128)(2,1)S(1)} %bitcast.8, bf16[128,1536]{1,0:T(8,128)(2,1)S(1)} %bitcast.10, bf16[8,1536]{1,0:T(8,128)(2,1)S(1)} %collective-permute-done.1.halo0_ref, ...), custom_call_target="tpu_custom_call" | custom-call | tf_op jit(solution)/shard_map/local/pallas_call | solution.py:257
  30.9 36.2 %all-gather = bf16[2560,128]{1,0:T(8,128)(2,1)S(1)} all-gather(bf16[160,128]{1,0:T(8,128)(2,1)S(1)} %get-tuple-element.20), channel_id=2, replica_groups={{0,48,64,112,128,176,192,240,256,304,320,368,384,432,448,496},{16,32,80..., dimensions={0}, use_global_device_ids=true | all-gather | bytes 696320 | tf_op jit(solution)/shard_map/all_gather | solution.py:276
  67.1 2.0 %chain.1.mine_ref = f32[128,128]{1,0:T(8,128)S(1)} custom-call(bf16[16,160,128]{2,1,0:T(8,128)(2,1)S(1)} %bitcast.7, bf16[2,128,128]{2,1,0:T(8,128)(2,1)S(1)} %get-tuple-element.21.qeff_ref, f32[2,96,128]{2,1,0:T(8,128)S(1)} %get-tuple-element.22.oeff_ref, f32[2,3,64,64]{3,2,1,0:T(8,128)S(1)} %copy-done.2), custom_call_target="tpu_custom_call" | custom-call | tf_op jit(solution)/shard_map/chain/pallas_call | solution.py:277
  69.0 1.9 %collective-permute-start.3 = (f32[128,128]{1,0:T(8,128)S(1)}, f32[128,128]{1,0:T(8,128)S(1)}, u32[]{:S(2)}, u32[]{:S(2)}) collective-permute-start(f32[128,128]{1,0:T(8,128)S(1)} %chain.1.mine_ref), channel_id=1, source_target_pairs={{0,16},{16,0},{32,48},{48,32},{64,80},{80,64},{96,112},{112,96},{1... | collective-permute-start | bytes 196616 | tf_op jit(solution)/shard_map/ppermute | solution.py:285
  71.0 1.2 %collective-permute-done.3.mate_ref = f32[128,128]{1,0:T(8,128)S(1)} collective-permute-done((f32[128,128]{1,0:T(8,128)S(1)}, f32[128,128]{1,0:T(8,128)S(1)}, u32[]{:S(2)}, u32[]{:S(2)}) %collective-permute-start.3) | collective-permute-done | bytes 65568 | tf_op jit(solution)/shard_map/ppermute | solution.py:285
  72.2 0.6 output.1
  72.8 12.5 %all_to_all.10.parts_ref = bf16[16,8,1536]{2,1,0:T(8,128)(2,1)S(1)} all-to-all(bf16[16,8,1536]{2,1,0:T(8,128)(2,1)S(1)} %bitcast.9), channel_id=1, replica_groups=mesh['seq'=32,'head'=16] {'head'}, dimensions={0} | all-to-all | bytes 786432 | tf_op jit(solution)/shard_map/all_to_all | solution.py:294
  85.3 0.7 total.1
  (9 shorter events, 0.0 us)
Async XLA Ops:
  0.0 0.7 copy-start.4
  1.5 15.6 %all-to-all-start = ((bf16[16,8,1536]{2,1,0:T(8,128)(2,1)}), bf16[16,8,1536]{2,1,0:T(8,128)(2,1)S(1)}, u32[]{:S(2)}, u32[]{:S(2)}) async-start(bf16[16,8,1536]{2,1,0:T(8,128)(2,1)} %fold.1), calls=%async_computation | async-start | bytes 786432 | tf_op jit(solution)/shard_map/all_to_all | solution.py:236
  9.1 2.0 %copy-start = (bf16[3,192,3072]{2,1,0:T(8,128)(2,1)S(1)}, bf16[3,192,3072]{2,1,0:T(8,128)(2,1)}, u32[]{:S(2)}) copy-start(bf16[3,192,3072]{2,1,0:T(8,128)(2,1)} %w_hbm.1) | copy-start | bytes 10616836
  11.1 0.7 copy-start.3
  11.9 0.7 copy-start.5
  12.6 0.7 copy-start.6
  13.5 53.5 %copy-start.2 = (f32[2,3,64,64]{3,2,1,0:T(8,128)S(1)}, f32[2,3,64,64]{3,2,1,0:T(8,128)}, u32[]{:S(2)}) copy-start(f32[2,3,64,64]{3,2,1,0:T(8,128)} %init_ref.1) | copy-start | bytes 294916
  17.1 10.5 %collective-permute-start = (bf16[16,8,1536]{2,1,0:T(8,128)(2,1)S(1)}, bf16[16,8,1536]{2,1,0:T(8,128)(2,1)S(1)}, u32[]{:S(2)}, u32[]{:S(2)}) collective-permute-start(bf16[16,8,1536]{2,1,0:T(8,128)(2,1)S(1)} %all-to-all-done), channel_id=1, source_target_pairs={{0,16},{16,0},{32,48},{48,32},{64,80},{80,64},{96,112},{112,96},{1... | collective-permute-start | bytes 1179656 | tf_op jit(solution)/shard_map/ppermute | solution.py:253
  23.0 3.7 %collective-permute-start.2 = (bf16[8,1536]{1,0:T(8,128)(2,1)S(1)}, bf16[8,1536]{1,0:T(8,128)(2,1)S(1)}, u32[]{:S(2)}, u32[]{:S(2)}) collective-permute-start(bf16[8,1536]{1,0:T(8,128)(2,1)S(1)} %slice_bitcast_fusion), channel_id=1, source_target_pairs={{16,48},{48,80},{80,112},{112,144},{144,176},{176,208},{208,240},{... | collective-permute-start | bytes 73736 | tf_op jit(solution)/shard_map/ppermute | solution.py:256
  25.4 2.2 %collective-permute-start.1 = (bf16[8,1536]{1,0:T(8,128)(2,1)S(1)}, bf16[8,1536]{1,0:T(8,128)(2,1)S(1)}, u32[]{:S(2)}, u32[]{:S(2)}) collective-permute-start(bf16[8,1536]{1,0:T(8,128)(2,1)S(1)} %slice_bitcast_fusion), channel_id=1, source_target_pairs={{16,32},{48,64},{80,96},{112,128},{144,160},{176,192},{208,224},{2... | collective-permute-start | bytes 73736 | tf_op jit(solution)/shard_map/ppermute | solution.py:255
  27.6 44.6 %copy-start.1 = (bf16[192,3072]{1,0:T(8,128)(2,1)S(1)}, bf16[192,3072]{1,0:T(8,128)(2,1)}, u32[]{:S(2)}) copy-start(bf16[192,3072]{1,0:T(8,128)(2,1)} %w_ref.1) | copy-start | bytes 3538948
  69.0 3.1 %collective-permute-start.3 = (f32[128,128]{1,0:T(8,128)S(1)}, f32[128,128]{1,0:T(8,128)S(1)}, u32[]{:S(2)}, u32[]{:S(2)}) collective-permute-start(f32[128,128]{1,0:T(8,128)S(1)} %chain.1.mine_ref), channel_id=1, source_target_pairs={{0,16},{16,0},{32,48},{48,32},{64,80},{80,64},{96,112},{112,96},{1... | collective-permute-start | bytes 196616 | tf_op jit(solution)/shard_map/ppermute | solution.py:285

commit v4 on v3

--- a/solution.py
+++ b/solution.py
@@ -110,39 +110,34 @@
     strict = dst // MB > src // MB
     eye = jnp.where(src == dst, 1.0, 0.0).astype(F32)
 
-    maps = []
-    for slot in range(2):
-        lo, hi = slot * 64, (slot + 1) * 64
-        q = convs[0][lo:hi]
-        k = convs[1][lo:hi]
-        k = k * lax.rsqrt((jnp.mean(k * k, axis=0, keepdims=True) + EPSILON) * 64)
-        rate = jax.nn.sigmoid(proj[352 + slot:353 + slot, 0:128]) * rate_ref[slot:slot + 1, :]
-        v = proj[256:320, 0:128] if slot == 0 else proj[320:352, 0:128]
-        kb = k.astype(BF16)
-        kt = kb.T
-        grams = mm(kt, cat([kb, q.astype(BF16)], 1))
-        u = jnp.where(strict, grams[:, 0:128], 0.0) * rate
-        ub = u.astype(BF16)
-        u2 = mm(ub, ub)
-        u2b = u2.astype(BF16)
-        u4 = mm(u2b, u2b)
-        t1 = eye - u + u2 - mm(ub, u2b)
-        t = t1 + mm(t1.astype(BF16), u4.astype(BF16))
-        rev = t.T * rate
-        fwd = rev.T
-        scores = grams[:, 128:256]
-        seen_f = jnp.where(dst >= src, scores, 0.0).astype(BF16)
-        seen_r = jnp.where(dst <= src, scores, 0.0).astype(BF16)
-        solved_f = mm(fwd.astype(BF16), cat([seen_f, kt], 1)).astype(BF16)
-        solved_r = mm(rev.astype(BF16), cat([seen_r, kt], 1)).astype(BF16)
-        stacked = cat([kb, v.astype(BF16)], 0)
-        pair = []
-        for way, solved in enumerate((solved_f, solved_r)):
-            both = mm(stacked, solved)
-            qeff_ref[way, lo:hi, :] = (q - both[0:64, 0:128]).astype(BF16)
-            oeff_ref[way, lo:lo + v.shape[0], :] = both[64:, 0:128]
-            pair.append((-both[0:64, 128:192], both[64:, 128:192]))
-        maps.append(pair)
+    two = range(2)
+    q = [convs[0][64 * i:64 * i + 64] for i in two]
+    k = [convs[1][64 * i:64 * i + 64] for i in two]
+    k = [x * lax.rsqrt((jnp.mean(x * x, axis=0, keepdims=True) + EPSILON) * 64) for x in k]
+    rate = [jax.nn.sigmoid(proj[352 + i:353 + i, 0:128]) * rate_ref[i:i + 1, :] for i in two]
+    v = [proj[256:320, 0:128], proj[320:352, 0:128]]
+    kb = [x.astype(BF16) for x in k]
+    kt = [x.T for x in kb]
+    grams = [mm(kt[i], cat([kb[i], q[i].astype(BF16)], 1)) for i in two]
+    u = [jnp.where(strict, grams[i][:, 0:128], 0.0) * rate[i] for i in two]
+    ub = [x.astype(BF16) for x in u]
+    u2 = [mm(x, x) for x in ub]
+    u2b = [x.astype(BF16) for x in u2]
+    u4 = [mm(x, x).astype(BF16) for x in u2b]
+    u3 = [mm(ub[i], u2b[i]) for i in two]
+    t1 = [eye - u[i] + u2[i] - u3[i] for i in two]
+    t = [t1[i] + mm(t1[i].astype(BF16), u4[i]) for i in two]
+    rev = [t[i].T * rate[i] for i in two]
+    ways = [[x.T.astype(BF16) for x in rev], [x.astype(BF16) for x in rev]]
+    seen = [[jnp.where(mask, grams[i][:, 128:256], 0.0).astype(BF16) for i in two] for mask in (dst >= src, dst <= src)]
+    solved = [[mm(ways[w][i], cat([seen[w][i], kt[i]], 1)).astype(BF16) for i in two] for w in two]
+    stacked = [cat([kb[i], v[i].astype(BF16)], 0) for i in two]
+    both = [[mm(stacked[i], solved[w][i]) for i in two] for w in two]
+    for w in two:
+        for i in two:
+            qeff_ref[w, 64 * i:64 * i + 64, :] = (q[i] - both[w][i][0:64, 0:128]).astype(BF16)
+            oeff_ref[w, 64 * i:64 * i + v[i].shape[0], :] = both[w][i][64:, 0:128]
+    maps = [[(-both[w][i][0:64, 128:192], both[w][i][64:, 128:192]) for w in two] for i in two]
     (a0, b0), (a1, b1) = maps[0][0], maps[1][0]
     send_ref[0:64, :] = cat([a0, a1], 1).astype(BF16)
     for way in range(2):

time: 86.5 us -> 85.7 us (level)
  no operation moved by 1% of the time
where the time goes in v4:
time: 85.7 us; the launch traced here: 85.2 us
  blocking collectives  48.7 us (57%)
  starting transfers between devices  19 us (22%)
  Pallas kernels  6.84 us (8%)
  waiting for transfers between devices  5.7 us (7%)
  local copies, waits for them, and re-layouts  4.83 us (6%)
    all_gather x1, blocking collectives, shards(): received = lax.all_gather(send, 'seq', axis_index_groups=groups)  36.2 us
    all_to_all x1, blocking collectives, shards(): parts = lax.all_to_all(partial.reshape(n_head, 8, half), 'head', 0, 0)  12.5 us
    all_to_all x1, starting transfers between devices, shards(): own = lax.all_to_all(folded, 'head', 0, 0)  7.58 us
    ppermute x1, starting transfers between devices, shards(): mate = lax.ppermute(own, 'seq', swap)  5.81 us
    unnamed x14, local copies, waits for them, and re-layouts  4.83 us
    all_to_all x1, waiting for transfers between devices, shards(): own = lax.all_to_all(folded, 'head', 0, 0)  3.58 us
    pallas_call x1, Pallas kernels, shards(): pl.pallas_call(local_kernel, out_shape=(jax.ShapeDtypeStruct((160, 128),...  2.46 us
    ppermute x1, starting transfers between devices, shards(): lax.ppermute(tail, 'seq', [(i, i + 2) for i in range(1, n_seq - 2, 2)])  2.4 us
  transfers between devices with their start and end apart: 5, of which 3 were waited for; matrix products, arithmetic and copies ran while one was open for 0% of the time, Pallas kernels for 0%

profile of v4, /device:TPU:1, one launch (start us, length us, event | category | flops | bytes accessed | tf_op | source)
XLA Modules:
  0.0 85.2 jit_solution(13437146213316851354)
XLA Ops:
  0.0 0.7 copy-done.4
  0.7 0.8 fold.1
  1.5 7.6 %all-to-all-start = ((bf16[16,8,1536]{2,1,0:T(8,128)(2,1)}), bf16[16,8,1536]{2,1,0:T(8,128)(2,1)S(1)}, u32[]{:S(2)}, u32[]{:S(2)}) async-start(bf16[16,8,1536]{2,1,0:T(8,128)(2,1)} %fold.1), calls=%async_computation | async-start | bytes 786432 | tf_op jit(solution)/shard_map/all_to_all | solution.py:231
  9.1 0.0 copy-start
  9.1 2.0 %copy-done = bf16[3,192,3072]{2,1,0:T(8,128)(2,1)S(1)} copy-done((bf16[3,192,3072]{2,1,0:T(8,128)(2,1)S(1)}, bf16[3,192,3072]{2,1,0:T(8,128)(2,1)}, u32[]{:S(2)}) %copy-start) | copy-done | bytes 3538968
  11.1 0.7 copy-done.3
  11.9 0.7 copy-done.5
  12.6 0.7 copy-done.6
  13.2 0.3 prepare.1
  13.5 0.0 copy-start.2
  13.6 3.6 %all-to-all-done = bf16[16,8,1536]{2,1,0:T(8,128)(2,1)S(1)} async-done(((bf16[16,8,1536]{2,1,0:T(8,128)(2,1)}), bf16[16,8,1536]{2,1,0:T(8,128)(2,1)S(1)}, u32[]{:S(2)}, u32[]{:S(2)}) %all-to-all-start) | async-done | bytes 393248 | tf_op jit(solution)/shard_map/all_to_all | solution.py:231
  17.1 5.8 %collective-permute-start = (bf16[16,8,1536]{2,1,0:T(8,128)(2,1)S(1)}, bf16[16,8,1536]{2,1,0:T(8,128)(2,1)S(1)}, u32[]{:S(2)}, u32[]{:S(2)}) collective-permute-start(bf16[16,8,1536]{2,1,0:T(8,128)(2,1)S(1)} %all-to-all-done), channel_id=1, source_target_pairs={{0,16},{16,0},{32,48},{48,32},{64,80},{80,64},{96,112},{112,96},{1... | collective-permute-start | bytes 1179656 | tf_op jit(solution)/shard_map/ppermute | solution.py:248
  23.0 2.4 %collective-permute-start.2 = (bf16[8,1536]{1,0:T(8,128)(2,1)S(1)}, bf16[8,1536]{1,0:T(8,128)(2,1)S(1)}, u32[]{:S(2)}, u32[]{:S(2)}) collective-permute-start(bf16[8,1536]{1,0:T(8,128)(2,1)S(1)} %slice_bitcast_fusion), channel_id=1, source_target_pairs={{16,48},{48,80},{80,112},{112,144},{144,176},{176,208},{208,240},{... | collective-permute-start | bytes 73736 | tf_op jit(solution)/shard_map/ppermute | solution.py:251
  25.4 1.3 %collective-permute-start.1 = (bf16[8,1536]{1,0:T(8,128)(2,1)S(1)}, bf16[8,1536]{1,0:T(8,128)(2,1)S(1)}, u32[]{:S(2)}, u32[]{:S(2)}) collective-permute-start(bf16[8,1536]{1,0:T(8,128)(2,1)S(1)} %slice_bitcast_fusion), channel_id=1, source_target_pairs={{16,32},{48,64},{80,96},{112,128},{144,160},{176,192},{208,224},{2... | collective-permute-start | bytes 73736 | tf_op jit(solution)/shard_map/ppermute | solution.py:250
  26.7 0.0 collective-permute-done.2.halo1_ref
  26.7 0.9 %collective-permute-done.1.halo0_ref = bf16[8,1536]{1,0:T(8,128)(2,1)S(1)} collective-permute-done((bf16[8,1536]{1,0:T(8,128)(2,1)S(1)}, bf16[8,1536]{1,0:T(8,128)(2,1)S(1)}, u32[]{:S(2)}, u32[]{:S(2)}) %collective-permute-start.1) | collective-permute-done | bytes 24608 | tf_op jit(solution)/shard_map/ppermute | solution.py:250
  27.6 2.5 %local.1 = (bf16[160,128]{1,0:T(8,128)(2,1)S(1)}, bf16[2,128,128]{2,1,0:T(8,128)(2,1)S(1)}, f32[2,96,128]{2,1,0:T(8,128)S(1)}) custom-call(bf16[128,1536]{1,0:T(8,128)(2,1)S(1)} %bitcast.8, bf16[128,1536]{1,0:T(8,128)(2,1)S(1)} %bitcast.10, bf16[8,1536]{1,0:T(8,128)(2,1)S(1)} %collective-permute-done.1.halo0_ref, ...), custom_call_target="tpu_custom_call" | custom-call | tf_op jit(solution)/shard_map/local/pallas_call | solution.py:252
  30.1 36.2 %all-gather = bf16[2560,128]{1,0:T(8,128)(2,1)S(1)} all-gather(bf16[160,128]{1,0:T(8,128)(2,1)S(1)} %get-tuple-element.20), channel_id=2, replica_groups={{0,48,64,112,128,176,192,240,256,304,320,368,384,432,448,496},{16,32,80..., dimensions={0}, use_global_device_ids=true | all-gather | bytes 696320 | tf_op jit(solution)/shard_map/all_gather | solution.py:271
  66.2 2.0 %chain.1.mine_ref = f32[128,128]{1,0:T(8,128)S(1)} custom-call(bf16[16,160,128]{2,1,0:T(8,128)(2,1)S(1)} %bitcast.7, bf16[2,128,128]{2,1,0:T(8,128)(2,1)S(1)} %get-tuple-element.21.qeff_ref, f32[2,96,128]{2,1,0:T(8,128)S(1)} %get-tuple-element.22.oeff_ref, f32[2,3,64,64]{3,2,1,0:T(8,128)S(1)} %copy-done.2), custom_call_target="tpu_custom_call" | custom-call | tf_op jit(solution)/shard_map/chain/pallas_call | solution.py:272
  68.2 1.9 %collective-permute-start.3 = (f32[128,128]{1,0:T(8,128)S(1)}, f32[128,128]{1,0:T(8,128)S(1)}, u32[]{:S(2)}, u32[]{:S(2)}) collective-permute-start(f32[128,128]{1,0:T(8,128)S(1)} %chain.1.mine_ref), channel_id=1, source_target_pairs={{0,16},{16,0},{32,48},{48,32},{64,80},{80,64},{96,112},{112,96},{1... | collective-permute-start | bytes 196616 | tf_op jit(solution)/shard_map/ppermute | solution.py:280
  70.2 1.2 %collective-permute-done.3.mate_ref = f32[128,128]{1,0:T(8,128)S(1)} collective-permute-done((f32[128,128]{1,0:T(8,128)S(1)}, f32[128,128]{1,0:T(8,128)S(1)}, u32[]{:S(2)}, u32[]{:S(2)}) %collective-permute-start.3) | collective-permute-done | bytes 65568 | tf_op jit(solution)/shard_map/ppermute | solution.py:280
  71.4 0.6 output.1
  72.0 12.5 %all_to_all.10.parts_ref = bf16[16,8,1536]{2,1,0:T(8,128)(2,1)S(1)} all-to-all(bf16[16,8,1536]{2,1,0:T(8,128)(2,1)S(1)} %bitcast.9), channel_id=1, replica_groups=mesh['seq'=32,'head'=16] {'head'}, dimensions={0} | all-to-all | bytes 786432 | tf_op jit(solution)/shard_map/all_to_all | solution.py:289
  84.5 0.7 total.1
  (9 shorter events, 0.0 us)
Async XLA Ops:
  0.0 0.7 copy-start.4
  1.5 15.6 %all-to-all-start = ((bf16[16,8,1536]{2,1,0:T(8,128)(2,1)}), bf16[16,8,1536]{2,1,0:T(8,128)(2,1)S(1)}, u32[]{:S(2)}, u32[]{:S(2)}) async-start(bf16[16,8,1536]{2,1,0:T(8,128)(2,1)} %fold.1), calls=%async_computation | async-start | bytes 786432 | tf_op jit(solution)/shard_map/all_to_all | solution.py:231
  9.1 2.0 %copy-start = (bf16[3,192,3072]{2,1,0:T(8,128)(2,1)S(1)}, bf16[3,192,3072]{2,1,0:T(8,128)(2,1)}, u32[]{:S(2)}) copy-start(bf16[3,192,3072]{2,1,0:T(8,128)(2,1)} %w_hbm.1) | copy-start | bytes 10616836
  11.1 0.7 copy-start.3
  11.9 0.7 copy-start.5
  12.6 0.7 copy-start.6
  13.5 52.7 %copy-start.2 = (f32[2,3,64,64]{3,2,1,0:T(8,128)S(1)}, f32[2,3,64,64]{3,2,1,0:T(8,128)}, u32[]{:S(2)}) copy-start(f32[2,3,64,64]{3,2,1,0:T(8,128)} %init_ref.1) | copy-start | bytes 294916
  17.1 10.5 %collective-permute-start = (bf16[16,8,1536]{2,1,0:T(8,128)(2,1)S(1)}, bf16[16,8,1536]{2,1,0:T(8,128)(2,1)S(1)}, u32[]{:S(2)}, u32[]{:S(2)}) collective-permute-start(bf16[16,8,1536]{2,1,0:T(8,128)(2,1)S(1)} %all-to-all-done), channel_id=1, source_target_pairs={{0,16},{16,0},{32,48},{48,32},{64,80},{80,64},{96,112},{112,96},{1... | collective-permute-start | bytes 1179656 | tf_op jit(solution)/shard_map/ppermute | solution.py:248
  23.0 3.7 %collective-permute-start.2 = (bf16[8,1536]{1,0:T(8,128)(2,1)S(1)}, bf16[8,1536]{1,0:T(8,128)(2,1)S(1)}, u32[]{:S(2)}, u32[]{:S(2)}) collective-permute-start(bf16[8,1536]{1,0:T(8,128)(2,1)S(1)} %slice_bitcast_fusion), channel_id=1, source_target_pairs={{16,48},{48,80},{80,112},{112,144},{144,176},{176,208},{208,240},{... | collective-permute-start | bytes 73736 | tf_op jit(solution)/shard_map/ppermute | solution.py:251
  25.4 2.2 %collective-permute-start.1 = (bf16[8,1536]{1,0:T(8,128)(2,1)S(1)}, bf16[8,1536]{1,0:T(8,128)(2,1)S(1)}, u32[]{:S(2)}, u32[]{:S(2)}) collective-permute-start(bf16[8,1536]{1,0:T(8,128)(2,1)S(1)} %slice_bitcast_fusion), channel_id=1, source_target_pairs={{16,32},{48,64},{80,96},{112,128},{144,160},{176,192},{208,224},{2... | collective-permute-start | bytes 73736 | tf_op jit(solution)/shard_map/ppermute | solution.py:250
  27.6 43.8 %copy-start.1 = (bf16[192,3072]{1,0:T(8,128)(2,1)S(1)}, bf16[192,3072]{1,0:T(8,128)(2,1)}, u32[]{:S(2)}) copy-start(bf16[192,3072]{1,0:T(8,128)(2,1)} %w_ref.1) | copy-start | bytes 3538948
  68.2 3.1 %collective-permute-start.3 = (f32[128,128]{1,0:T(8,128)S(1)}, f32[128,128]{1,0:T(8,128)S(1)}, u32[]{:S(2)}, u32[]{:S(2)}) collective-permute-start(f32[128,128]{1,0:T(8,128)S(1)} %chain.1.mine_ref), channel_id=1, source_target_pairs={{0,16},{16,0},{32,48},{48,32},{64,80},{80,64},{96,112},{112,96},{1... | collective-permute-start | bytes 196616 | tf_op jit(solution)/shard_map/ppermute | solution.py:280

commit v5 on v4

--- a/solution.py
+++ b/solution.py
@@ -68,21 +68,26 @@
             out_ref[pl.ds(row, 64), cols] = wide_ref[j, pl.ds(part, 64, stride=2), :].astype(BF16)
 
 
-def local_kernel(own_ref, mate_ref, halo0_ref, halo1_ref, w_ref, lrp_ref, taps_ref, rate_ref,
-                 send_ref, qeff_ref, oeff_ref, wide_ref, tail_ref, xall_ref):
+def tail_kernel(halo0_ref, halo1_ref, out_ref, wide_ref):
+    core = lax.axis_index("seq") % 2
+    half = halo0_ref.shape[1]
+    halo = jnp.where(core == 0, halo0_ref[...].astype(F32), halo1_ref[...].astype(F32))
+    for j in range(half // 128):
+        wide_ref[j, 0:24, :] = jnp.zeros((24, 128), F32)
+        wide_ref[j, 24:32, :] = halo[:, j * 128:(j + 1) * 128]
+        for part in range(2):
+            cols = slice(part * half + j * 128, part * half + (j + 1) * 128)
+            out_ref[:, cols] = wide_ref[j, pl.ds(part, 16, stride=2), :].astype(BF16)
+
+
+def local_kernel(own_ref, mate_ref, tail_ref, w_ref, lrp_ref, taps_ref, rate_ref,
+                 send_ref, qeff_ref, oeff_ref, wide_ref, xall_ref):
     place = lax.axis_index("seq")
     core = place % 2
     role = role_of(place)
-    half = halo0_ref.shape[1]
     spread(own_ref, wide_ref, xall_ref, pl.multiple_of(64 * core, 64))
     spread(mate_ref, wide_ref, xall_ref, pl.multiple_of(64 * (1 - core), 64))
-    halo = jnp.where(core == 0, halo0_ref[...].astype(F32), halo1_ref[...].astype(F32))
-    for j in range(half // 128):
-        tail_ref[j, 0:24, :] = jnp.zeros((24, 128), F32)
-        tail_ref[j, 24:32, :] = halo[:, j * 128:(j + 1) * 128]
-        for part in range(2):
-            cols = slice(part * half + j * 128, part * half + (j + 1) * 128)
-            xall_ref[240:256, cols] = tail_ref[j, pl.ds(part, 16, stride=2), :].astype(BF16)
+    xall_ref[240:256, :] = tail_ref[...]
     at = pl.multiple_of(128 * role, 64)
     whole = pl.ds(pl.multiple_of(64 * role, 64), 64)
     shared = pl.ds(pl.multiple_of(64 * (1 - role), 64), 64)
@@ -249,6 +254,16 @@
     tail = own[n_head - 1]
     halo0 = lax.ppermute(tail, "seq", [(i, i + 1) for i in range(1, n_seq - 1, 2)])
     halo1 = lax.ppermute(tail, "seq", [(i, i + 2) for i in range(1, n_seq - 2, 2)])
+    tails = pl.pallas_call(
+        tail_kernel,
+        out_shape=jax.ShapeDtypeStruct((16, width), BF16),
+        in_specs=[vmem] * 2,
+        out_specs=vmem,
+        scratch_shapes=[pltpu.VMEM((half // 128, 32, 128), F32)],
+        compiler_params=params,
+        cost_estimate=pl.CostEstimate(flops=20_000_000_000, transcendentals=0, bytes_accessed=0),
+        name="tails",
+    )(halo0, halo1)
     send, qeff, oeff = pl.pallas_call(
         local_kernel,
         out_shape=(
@@ -256,16 +271,15 @@
             jax.ShapeDtypeStruct((2, 128, 128), BF16),
             jax.ShapeDtypeStruct((2, 96, 128), F32),
         ),
-        in_specs=[vmem] * 8,
+        in_specs=[vmem] * 7,
         out_specs=(vmem, vmem, vmem),
         scratch_shapes=[
             pltpu.VMEM((half // 128, 128, 128), F32),
-            pltpu.VMEM((half // 128, 32, 128), F32),
             pltpu.VMEM((256, width), BF16),
         ],
         compiler_params=params,
         name="local",
-    )(own.reshape(n_head * 8, half), mate.reshape(n_head * 8, half), halo0, halo1, weights, lr_rows, taps, base)
+    )(own.reshape(n_head * 8, half), mate.reshape(n_head * 8, half), tails, weights, lr_rows, taps, base)
 
     groups = [[2 * j + (c + j) % 2 for j in range(n_seq // 2)] for c in range(2)]
     received = lax.all_gather(send, "seq", axis_index_groups=groups)

time: 85.7 us -> 83.6 us (0.975)
  blocking collectives: 48.7 us -> 46.6 us
    ppermute x1, starting transfers between devices: 5.81 us -> 1.92 us  [shards(): mate = lax.ppermute(own, 'seq', swap)]
    all_gather x1, blocking collectives: 36.2 us -> 34 us  [shards(): received = lax.all_gather(send, 'seq', axis_index_groups=groups)]
    ppermute x1, starting transfers between devices: 1.29 us -> 3.06 us  [shards(): lax.ppermute(tail, 'seq', [(i, i + 1) for i in range(1, n_seq - 1, 2)])]
    ppermute x1, waiting for transfers between devices: 0.01 us -> 1.61 us  [shards(): mate = lax.ppermute(own, 'seq', swap)]
    ppermute x1, starting transfers between devices: 2.4 us -> 3.79 us  [shards(): lax.ppermute(tail, 'seq', [(i, i + 2) for i in range(1, n_seq - 2, 2)])]
    ppermute x1, waiting for transfers between devices: 0.92 us -> 0.01 us  [shards(): lax.ppermute(tail, 'seq', [(i, i + 1) for i in range(1, n_seq - 1, 2)])]
where the time goes in v5:
time: 83.6 us; the launch traced here: 83 us
  blocking collectives  46.6 us (56%)
  starting transfers between devices  18.4 us (22%)
  Pallas kernels  6.84 us (8%)
  waiting for transfers between devices  6.32 us (8%)
  local copies, waits for them, and re-layouts  4.83 us (6%)
    all_gather x1, blocking collectives, shards(): received = lax.all_gather(send, 'seq', axis_index_groups=groups)  34 us
    all_to_all x1, blocking collectives, shards(): parts = lax.all_to_all(partial.reshape(n_head, 8, half), 'head', 0, 0)  12.6 us
    all_to_all x1, starting transfers between devices, shards(): own = lax.all_to_all(folded, 'head', 0, 0)  7.58 us
    unnamed x14, local copies, waits for them, and re-layouts  4.83 us
    ppermute x1, starting transfers between devices, shards(): lax.ppermute(tail, 'seq', [(i, i + 2) for i in range(1, n_seq - 2, 2)])  3.79 us
    all_to_all x1, waiting for transfers between devices, shards(): own = lax.all_to_all(folded, 'head', 0, 0)  3.59 us
    ppermute x1, starting transfers between devices, shards(): lax.ppermute(tail, 'seq', [(i, i + 1) for i in range(1, n_seq - 1, 2)])  3.06 us
    pallas_call x1, Pallas kernels, shards(): pl.pallas_call(local_kernel, out_shape=(jax.ShapeDtypeStruct((160, 128),...  2.44 us
  transfers between devices with their start and end apart: 5, of which 3 were waited for; matrix products, arithmetic and copies ran while one was open for 0% of the time, Pallas kernels for 0%

profile of v5, /device:TPU:1, one launch (start us, length us, event | category | flops | bytes accessed | tf_op | source)
XLA Modules:
  0.0 83.0 jit_solution(86747363339956447)
XLA Ops:
  0.0 0.7 copy-done.4
  0.7 0.8 fold.1
  1.5 7.6 %all-to-all-start = ((bf16[16,8,1536]{2,1,0:T(8,128)(2,1)}), bf16[16,8,1536]{2,1,0:T(8,128)(2,1)S(1)}, u32[]{:S(2)}, u32[]{:S(2)}) async-start(bf16[16,8,1536]{2,1,0:T(8,128)(2,1)} %fold.1), calls=%async_computation | async-start | bytes 786432 | tf_op jit(solution)/shard_map/all_to_all | solution.py:236
  9.1 0.0 copy-start
  9.1 2.0 %copy-done = bf16[3,192,3072]{2,1,0:T(8,128)(2,1)S(1)} copy-done((bf16[3,192,3072]{2,1,0:T(8,128)(2,1)S(1)}, bf16[3,192,3072]{2,1,0:T(8,128)(2,1)}, u32[]{:S(2)}) %copy-start) | copy-done | bytes 3538968
  11.1 0.7 copy-done.3
  11.9 0.7 copy-done.5
  12.6 0.7 copy-done.6
  13.2 0.3 prepare.1
  13.5 3.6 %all-to-all-done = bf16[16,8,1536]{2,1,0:T(8,128)(2,1)S(1)} async-done(((bf16[16,8,1536]{2,1,0:T(8,128)(2,1)}), bf16[16,8,1536]{2,1,0:T(8,128)(2,1)S(1)}, u32[]{:S(2)}, u32[]{:S(2)}) %all-to-all-start) | async-done | bytes 393248 | tf_op jit(solution)/shard_map/all_to_all | solution.py:236
  17.1 3.8 %collective-permute-start.2 = (bf16[8,1536]{1,0:T(8,128)(2,1)S(1)}, bf16[8,1536]{1,0:T(8,128)(2,1)S(1)}, u32[]{:S(2)}, u32[]{:S(2)}) collective-permute-start(bf16[8,1536]{1,0:T(8,128)(2,1)S(1)} %slice_bitcast_fusion), channel_id=1, source_target_pairs={{16,48},{48,80},{80,112},{112,144},{144,176},{176,208},{208,240},{... | collective-permute-start | bytes 73736 | tf_op jit(solution)/shard_map/ppermute | solution.py:256
  20.9 3.1 %collective-permute-start.1 = (bf16[8,1536]{1,0:T(8,128)(2,1)S(1)}, bf16[8,1536]{1,0:T(8,128)(2,1)S(1)}, u32[]{:S(2)}, u32[]{:S(2)}) collective-permute-start(bf16[8,1536]{1,0:T(8,128)(2,1)S(1)} %slice_bitcast_fusion), channel_id=1, source_target_pairs={{16,32},{48,64},{80,96},{112,128},{144,160},{176,192},{208,224},{2... | collective-permute-start | bytes 73736 | tf_op jit(solution)/shard_map/ppermute | solution.py:255
  24.0 1.9 %collective-permute-start = (bf16[16,8,1536]{2,1,0:T(8,128)(2,1)S(1)}, bf16[16,8,1536]{2,1,0:T(8,128)(2,1)S(1)}, u32[]{:S(2)}, u32[]{:S(2)}) collective-permute-start(bf16[16,8,1536]{2,1,0:T(8,128)(2,1)S(1)} %all-to-all-done), channel_id=1, source_target_pairs={{0,16},{16,0},{32,48},{48,32},{64,80},{80,64},{96,112},{112,96},{1... | collective-permute-start | bytes 1179656 | tf_op jit(solution)/shard_map/ppermute | solution.py:253
  25.9 0.0 collective-permute-done.2.halo1_ref
  26.0 0.0 copy-start.2
  26.0 1.6 %collective-permute-done = bf16[16,8,1536]{2,1,0:T(8,128)(2,1)S(1)} collective-permute-done((bf16[16,8,1536]{2,1,0:T(8,128)(2,1)S(1)}, bf16[16,8,1536]{2,1,0:T(8,128)(2,1)S(1)}, u32[]{:S(2)}, u32[]{:S(2)}) %collective-permute-start) | collective-permute-done | bytes 393248 | tf_op jit(solution)/shard_map/ppermute | solution.py:253
  27.6 2.4 %local.1 = (bf16[160,128]{1,0:T(8,128)(2,1)S(1)}, bf16[2,128,128]{2,1,0:T(8,128)(2,1)S(1)}, f32[2,96,128]{2,1,0:T(8,128)S(1)}) custom-call(bf16[128,1536]{1,0:T(8,128)(2,1)S(1)} %bitcast.8, bf16[128,1536]{1,0:T(8,128)(2,1)S(1)} %bitcast.10, bf16[16,3072]{1,0:T(8,128)(2,1)S(1)} %tails.1.tail_ref, bf16[3,128,3072]{2,1,0:T(8,128)(2,1)S(1)} %get-tuple-element.16.w_ref, ...), custom_call_target="tpu_custom_call" | custom-call | tf_op jit(solution)/shard_map/local/pallas_call | solution.py:267
  30.1 34.0 %all-gather = bf16[2560,128]{1,0:T(8,128)(2,1)S(1)} all-gather(bf16[160,128]{1,0:T(8,128)(2,1)S(1)} %get-tuple-element.20), channel_id=2, replica_groups={{0,48,64,112,128,176,192,240,256,304,320,368,384,432,448,496},{16,32,80..., dimensions={0}, use_global_device_ids=true | all-gather | bytes 696320 | tf_op jit(solution)/shard_map/all_gather | solution.py:285
  64.1 2.0 %chain.1.mine_ref = f32[128,128]{1,0:T(8,128)S(1)} custom-call(bf16[16,160,128]{2,1,0:T(8,128)(2,1)S(1)} %bitcast.7, bf16[2,128,128]{2,1,0:T(8,128)(2,1)S(1)} %get-tuple-element.21.qeff_ref, f32[2,96,128]{2,1,0:T(8,128)S(1)} %get-tuple-element.22.oeff_ref, f32[2,3,64,64]{3,2,1,0:T(8,128)S(1)} %copy-done.2), custom_call_target="tpu_custom_call" | custom-call | tf_op jit(solution)/shard_map/chain/pallas_call | solution.py:286
  66.1 2.0 %collective-permute-start.3 = (f32[128,128]{1,0:T(8,128)S(1)}, f32[128,128]{1,0:T(8,128)S(1)}, u32[]{:S(2)}, u32[]{:S(2)}) collective-permute-start(f32[128,128]{1,0:T(8,128)S(1)} %chain.1.mine_ref), channel_id=1, source_target_pairs={{0,16},{16,0},{32,48},{48,32},{64,80},{80,64},{96,112},{112,96},{1... | collective-permute-start | bytes 196616 | tf_op jit(solution)/shard_map/ppermute | solution.py:294
  68.1 1.1 %collective-permute-done.3.mate_ref = f32[128,128]{1,0:T(8,128)S(1)} collective-permute-done((f32[128,128]{1,0:T(8,128)S(1)}, f32[128,128]{1,0:T(8,128)S(1)}, u32[]{:S(2)}, u32[]{:S(2)}) %collective-permute-start.3) | collective-permute-done | bytes 65568 | tf_op jit(solution)/shard_map/ppermute | solution.py:294
  69.2 0.6 output.1
  69.8 12.6 %all_to_all.10.parts_ref = bf16[16,8,1536]{2,1,0:T(8,128)(2,1)S(1)} all-to-all(bf16[16,8,1536]{2,1,0:T(8,128)(2,1)S(1)} %bitcast.9), channel_id=1, replica_groups=mesh['seq'=32,'head'=16] {'head'}, dimensions={0} | all-to-all | bytes 786432 | tf_op jit(solution)/shard_map/all_to_all | solution.py:303
  82.4 0.7 total.1
  (10 shorter events, 0.1 us)
Async XLA Ops:
  0.0 0.7 copy-start.4
  1.5 15.6 %all-to-all-start = ((bf16[16,8,1536]{2,1,0:T(8,128)(2,1)}), bf16[16,8,1536]{2,1,0:T(8,128)(2,1)S(1)}, u32[]{:S(2)}, u32[]{:S(2)}) async-start(bf16[16,8,1536]{2,1,0:T(8,128)(2,1)} %fold.1), calls=%async_computation | async-start | bytes 786432 | tf_op jit(solution)/shard_map/all_to_all | solution.py:236
  9.1 2.0 %copy-start = (bf16[3,192,3072]{2,1,0:T(8,128)(2,1)S(1)}, bf16[3,192,3072]{2,1,0:T(8,128)(2,1)}, u32[]{:S(2)}) copy-start(bf16[3,192,3072]{2,1,0:T(8,128)(2,1)} %w_hbm.1) | copy-start | bytes 10616836
  11.1 0.7 copy-start.3
  11.9 0.7 copy-start.5
  12.6 0.7 copy-start.6
  17.1 8.8 %collective-permute-start.2 = (bf16[8,1536]{1,0:T(8,128)(2,1)S(1)}, bf16[8,1536]{1,0:T(8,128)(2,1)S(1)}, u32[]{:S(2)}, u32[]{:S(2)}) collective-permute-start(bf16[8,1536]{1,0:T(8,128)(2,1)S(1)} %slice_bitcast_fusion), channel_id=1, source_target_pairs={{16,48},{48,80},{80,112},{112,144},{144,176},{176,208},{208,240},{... | collective-permute-start | bytes 73736 | tf_op jit(solution)/shard_map/ppermute | solution.py:256
  20.9 5.0 %collective-permute-start.1 = (bf16[8,1536]{1,0:T(8,128)(2,1)S(1)}, bf16[8,1536]{1,0:T(8,128)(2,1)S(1)}, u32[]{:S(2)}, u32[]{:S(2)}) collective-permute-start(bf16[8,1536]{1,0:T(8,128)(2,1)S(1)} %slice_bitcast_fusion), channel_id=1, source_target_pairs={{16,32},{48,64},{80,96},{112,128},{144,160},{176,192},{208,224},{2... | collective-permute-start | bytes 73736 | tf_op jit(solution)/shard_map/ppermute | solution.py:255
  24.0 3.6 %collective-permute-start = (bf16[16,8,1536]{2,1,0:T(8,128)(2,1)S(1)}, bf16[16,8,1536]{2,1,0:T(8,128)(2,1)S(1)}, u32[]{:S(2)}, u32[]{:S(2)}) collective-permute-start(bf16[16,8,1536]{2,1,0:T(8,128)(2,1)S(1)} %all-to-all-done), channel_id=1, source_target_pairs={{0,16},{16,0},{32,48},{48,32},{64,80},{80,64},{96,112},{112,96},{1... | collective-permute-start | bytes 1179656 | tf_op jit(solution)/shard_map/ppermute | solution.py:253
  26.0 38.1 %copy-start.2 = (f32[2,3,64,64]{3,2,1,0:T(8,128)S(1)}, f32[2,3,64,64]{3,2,1,0:T(8,128)}, u32[]{:S(2)}) copy-start(f32[2,3,64,64]{3,2,1,0:T(8,128)} %init_ref.1) | copy-start | bytes 294916
  27.6 41.6 %copy-start.1 = (bf16[192,3072]{1,0:T(8,128)(2,1)S(1)}, bf16[192,3072]{1,0:T(8,128)(2,1)}, u32[]{:S(2)}) copy-start(bf16[192,3072]{1,0:T(8,128)(2,1)} %w_ref.1) | copy-start | bytes 3538948
  66.1 3.1 %collective-permute-start.3 = (f32[128,128]{1,0:T(8,128)S(1)}, f32[128,128]{1,0:T(8,128)S(1)}, u32[]{:S(2)}, u32[]{:S(2)}) collective-permute-start(f32[128,128]{1,0:T(8,128)S(1)} %chain.1.mine_ref), channel_id=1, source_target_pairs={{0,16},{16,0},{32,48},{48,32},{64,80},{80,64},{96,112},{112,96},{1... | collective-permute-start | bytes 196616 | tf_op jit(solution)/shard_map/ppermute | solution.py:294

commit v6 on v5

--- a/solution.py
+++ b/solution.py
@@ -29,16 +29,18 @@
     return (place + place // 2) % 2
 
 
-def fold_kernel(tokens_ref, out_ref, wide_ref):
-    half = out_ref.shape[2]
+def fold_kernel(tokens_ref, out_hbm, wide_ref, block_ref, sems):
+    half = block_ref.shape[1]
     for j in range(half // 128):
-        cols = slice(j * 128, (j + 1) * 128)
         for part in range(2):
             piece = tokens_ref[:, part * half + j * 128:part * half + (j + 1) * 128].astype(F32)
             wide_ref[j, pl.ds(part, 4, stride=2), :] = piece
-        block = wide_ref[j].astype(BF16)
-        for i in range(out_ref.shape[0]):
-            out_ref[i, :, cols] = block
+        block_ref[:, j * 128:(j + 1) * 128] = wide_ref[j].astype(BF16)
+    copies = [pltpu.make_async_copy(block_ref, out_hbm.at[i], sems.at[i]) for i in range(out_hbm.shape[0])]
+    for c in copies:
+        c.start()
+    for c in copies:
+        c.wait()
 
 
 def prepare_kernel(w_hbm, lrw_ref, conv_ref, base_ref, w_ref, lrp_ref, taps_ref, rate_ref, sem):
@@ -164,14 +166,15 @@
         for way in range(2):
             j = i if way == 0 else chips - 1 - i
             live = (j < chip) if way == 0 else (j > chip)
-            block = maps_ref[j]
+            block = jnp.where(live, maps_ref[j].astype(F32), 0.0)
             whole, shared = states[way]
             at = 64 + 48 * way
-            b0 = cat([block[at:at + 48, 0:64], block[at:at + 16, 64:128]], 0).astype(F32)
-            b1 = block[at + 16:at + 48, 64:128].astype(F32)
-            new0 = whole + mm(whole.astype(BF16), block[0:64, 0:64], 1, way) + b0
-            new1 = shared + mm(shared.astype(BF16), block[0:64, 64:128], 1, way) + b1
-            states[way] = [jnp.where(live, new0, whole), jnp.where(live, new1, shared)]
+            steps = block[0:64].astype(BF16)
+            b0 = cat([block[at:at + 48, 0:64], block[at:at + 16, 64:128]], 0)
+            b1 = block[at + 16:at + 48, 64:128]
+            new0 = (whole + b0) + mm(whole.astype(BF16), steps[:, 0:64], 1, way)
+            new1 = (shared + b1) + mm(shared.astype(BF16), steps[:, 64:128], 1, way)
+            states[way] = [new0, new1]
     sums = None
     for way in range(2):
         whole = mm(states[way][0].astype(BF16), qeff_ref[way, 0:64, :]) + oeff_ref[way, 0:64, :]
@@ -228,8 +231,12 @@
         fold_kernel,
         out_shape=jax.ShapeDtypeStruct((n_head, 8, half), BF16),
         in_specs=[vmem],
-        out_specs=vmem,
-        scratch_shapes=[pltpu.VMEM((half // 128, 8, 128), F32)],
+        out_specs=hbm,
+        scratch_shapes=[
+            pltpu.VMEM((half // 128, 8, 128), F32),
+            pltpu.VMEM((8, half), BF16),
+            pltpu.SemaphoreType.DMA((n_head,)),
+        ],
         compiler_params=params,
         name="fold",
     )(tokens)

time: 83.6 us -> 83.6 us (level)
  no operation moved by 1% of the time
where the time goes in v6:
time: 83.6 us; the launch traced here: 83.1 us
  blocking collectives  46.5 us (56%)
  starting transfers between devices  18.4 us (22%)
  Pallas kernels  6.91 us (8%)
  waiting for transfers between devices  6.32 us (8%)
  local copies, waits for them, and re-layouts  4.83 us (6%)
    all_gather x1, blocking collectives, shards(): received = lax.all_gather(send, 'seq', axis_index_groups=groups)  34 us
    all_to_all x1, blocking collectives, shards(): parts = lax.all_to_all(partial.reshape(n_head, 8, half), 'head', 0, 0)  12.5 us
    all_to_all x1, starting transfers between devices, shards(): own = lax.all_to_all(folded, 'head', 0, 0)  7.6 us
    unnamed x14, local copies, waits for them, and re-layouts  4.83 us
    ppermute x1, starting transfers between devices, shards(): lax.ppermute(tail, 'seq', [(i, i + 2) for i in range(1, n_seq - 2, 2)])  3.79 us
    all_to_all x1, waiting for transfers between devices, shards(): own = lax.all_to_all(folded, 'head', 0, 0)  3.59 us
    ppermute x1, starting transfers between devices, shards(): lax.ppermute(tail, 'seq', [(i, i + 1) for i in range(1, n_seq - 1, 2)])  3.06 us
    pallas_call x1, Pallas kernels, shards(): pl.pallas_call(local_kernel, out_shape=(jax.ShapeDtypeStruct((160, 128),...  2.44 us
  transfers between devices with their start and end apart: 5, of which 3 were waited for; matrix products, arithmetic and copies ran while one was open for 0% of the time, Pallas kernels for 0%

profile of v6, /device:TPU:1, one launch (start us, length us, event | category | flops | bytes accessed | tf_op | source)
XLA Modules:
  0.0 83.1 jit_solution(17229111206414756775)
XLA Ops:
  0.0 0.7 copy-done.4
  0.7 0.9 %fold.1 = bf16[16,8,1536]{2,1,0:T(8,128)(2,1)} custom-call(bf16[4,3072]{1,0:T(4,128)(2,1)S(1)} %copy-done.4), custom_call_target="tpu_custom_call" | custom-call | tf_op jit(solution)/shard_map/fold/pallas_call | solution.py:230
  1.6 7.6 %all-to-all-start = ((bf16[16,8,1536]{2,1,0:T(8,128)(2,1)}), bf16[16,8,1536]{2,1,0:T(8,128)(2,1)S(1)}, u32[]{:S(2)}, u32[]{:S(2)}) async-start(bf16[16,8,1536]{2,1,0:T(8,128)(2,1)} %fold.1), calls=%async_computation | async-start | bytes 786432 | tf_op jit(solution)/shard_map/all_to_all | solution.py:243
  9.3 0.0 copy-start
  9.3 2.0 %copy-done = bf16[3,192,3072]{2,1,0:T(8,128)(2,1)S(1)} copy-done((bf16[3,192,3072]{2,1,0:T(8,128)(2,1)S(1)}, bf16[3,192,3072]{2,1,0:T(8,128)(2,1)}, u32[]{:S(2)}) %copy-start) | copy-done | bytes 3538968
  11.3 0.7 copy-done.3
  12.0 0.7 copy-done.5
  12.7 0.7 copy-done.6
  13.3 0.3 prepare.1
  13.7 3.6 %all-to-all-done = bf16[16,8,1536]{2,1,0:T(8,128)(2,1)S(1)} async-done(((bf16[16,8,1536]{2,1,0:T(8,128)(2,1)}), bf16[16,8,1536]{2,1,0:T(8,128)(2,1)S(1)}, u32[]{:S(2)}, u32[]{:S(2)}) %all-to-all-start) | async-done | bytes 393248 | tf_op jit(solution)/shard_map/all_to_all | solution.py:243
  17.3 3.8 %collective-permute-start.2 = (bf16[8,1536]{1,0:T(8,128)(2,1)S(1)}, bf16[8,1536]{1,0:T(8,128)(2,1)S(1)}, u32[]{:S(2)}, u32[]{:S(2)}) collective-permute-start(bf16[8,1536]{1,0:T(8,128)(2,1)S(1)} %slice_bitcast_fusion), channel_id=1, source_target_pairs={{16,48},{48,80},{80,112},{112,144},{144,176},{176,208},{208,240},{... | collective-permute-start | bytes 73736 | tf_op jit(solution)/shard_map/ppermute | solution.py:263
  21.1 3.1 %collective-permute-start.1 = (bf16[8,1536]{1,0:T(8,128)(2,1)S(1)}, bf16[8,1536]{1,0:T(8,128)(2,1)S(1)}, u32[]{:S(2)}, u32[]{:S(2)}) collective-permute-start(bf16[8,1536]{1,0:T(8,128)(2,1)S(1)} %slice_bitcast_fusion), channel_id=1, source_target_pairs={{16,32},{48,64},{80,96},{112,128},{144,160},{176,192},{208,224},{2... | collective-permute-start | bytes 73736 | tf_op jit(solution)/shard_map/ppermute | solution.py:262
  24.1 1.9 %collective-permute-start = (bf16[16,8,1536]{2,1,0:T(8,128)(2,1)S(1)}, bf16[16,8,1536]{2,1,0:T(8,128)(2,1)S(1)}, u32[]{:S(2)}, u32[]{:S(2)}) collective-permute-start(bf16[16,8,1536]{2,1,0:T(8,128)(2,1)S(1)} %all-to-all-done), channel_id=1, source_target_pairs={{0,16},{16,0},{32,48},{48,32},{64,80},{80,64},{96,112},{112,96},{1... | collective-permute-start | bytes 1179656 | tf_op jit(solution)/shard_map/ppermute | solution.py:260
  26.1 0.0 collective-permute-done.2.halo1_ref
  26.1 0.0 copy-start.2
  26.1 1.6 %collective-permute-done = bf16[16,8,1536]{2,1,0:T(8,128)(2,1)S(1)} collective-permute-done((bf16[16,8,1536]{2,1,0:T(8,128)(2,1)S(1)}, bf16[16,8,1536]{2,1,0:T(8,128)(2,1)S(1)}, u32[]{:S(2)}, u32[]{:S(2)}) %collective-permute-start) | collective-permute-done | bytes 393248 | tf_op jit(solution)/shard_map/ppermute | solution.py:260
  27.7 2.4 %local.1 = (bf16[160,128]{1,0:T(8,128)(2,1)S(1)}, bf16[2,128,128]{2,1,0:T(8,128)(2,1)S(1)}, f32[2,96,128]{2,1,0:T(8,128)S(1)}) custom-call(bf16[128,1536]{1,0:T(8,128)(2,1)S(1)} %bitcast.8, bf16[128,1536]{1,0:T(8,128)(2,1)S(1)} %bitcast.10, bf16[16,3072]{1,0:T(8,128)(2,1)S(1)} %tails.1.tail_ref, bf16[3,128,3072]{2,1,0:T(8,128)(2,1)S(1)} %get-tuple-element.16.w_ref, ...), custom_call_target="tpu_custom_call" | custom-call | tf_op jit(solution)/shard_map/local/pallas_call | solution.py:274
  30.2 34.0 %all-gather = bf16[2560,128]{1,0:T(8,128)(2,1)S(1)} all-gather(bf16[160,128]{1,0:T(8,128)(2,1)S(1)} %get-tuple-element.20), channel_id=2, replica_groups={{0,48,64,112,128,176,192,240,256,304,320,368,384,432,448,496},{16,32,80..., dimensions={0}, use_global_device_ids=true | all-gather | bytes 696320 | tf_op jit(solution)/shard_map/all_gather | solution.py:292
  64.2 2.0 %chain.1.mine_ref = f32[128,128]{1,0:T(8,128)S(1)} custom-call(bf16[16,160,128]{2,1,0:T(8,128)(2,1)S(1)} %bitcast.7, bf16[2,128,128]{2,1,0:T(8,128)(2,1)S(1)} %get-tuple-element.21.qeff_ref, f32[2,96,128]{2,1,0:T(8,128)S(1)} %get-tuple-element.22.oeff_ref, f32[2,3,64,64]{3,2,1,0:T(8,128)S(1)} %copy-done.2), custom_call_target="tpu_custom_call" | custom-call | tf_op jit(solution)/shard_map/chain/pallas_call | solution.py:293
  66.2 2.0 %collective-permute-start.3 = (f32[128,128]{1,0:T(8,128)S(1)}, f32[128,128]{1,0:T(8,128)S(1)}, u32[]{:S(2)}, u32[]{:S(2)}) collective-permute-start(f32[128,128]{1,0:T(8,128)S(1)} %chain.1.mine_ref), channel_id=1, source_target_pairs={{0,16},{16,0},{32,48},{48,32},{64,80},{80,64},{96,112},{112,96},{1... | collective-permute-start | bytes 196616 | tf_op jit(solution)/shard_map/ppermute | solution.py:301
  68.2 1.1 %collective-permute-done.3.mate_ref = f32[128,128]{1,0:T(8,128)S(1)} collective-permute-done((f32[128,128]{1,0:T(8,128)S(1)}, f32[128,128]{1,0:T(8,128)S(1)}, u32[]{:S(2)}, u32[]{:S(2)}) %collective-permute-start.3) | collective-permute-done | bytes 65568 | tf_op jit(solution)/shard_map/ppermute | solution.py:301
  69.3 0.6 output.1
  69.9 12.5 %all_to_all.10.parts_ref = bf16[16,8,1536]{2,1,0:T(8,128)(2,1)S(1)} all-to-all(bf16[16,8,1536]{2,1,0:T(8,128)(2,1)S(1)} %bitcast.9), channel_id=1, replica_groups=mesh['seq'=32,'head'=16] {'head'}, dimensions={0} | all-to-all | bytes 786432 | tf_op jit(solution)/shard_map/all_to_all | solution.py:310
  82.4 0.7 total.1
  (10 shorter events, 0.1 us)
Async XLA Ops:
  0.0 0.7 copy-start.4
  1.6 15.6 %all-to-all-start = ((bf16[16,8,1536]{2,1,0:T(8,128)(2,1)}), bf16[16,8,1536]{2,1,0:T(8,128)(2,1)S(1)}, u32[]{:S(2)}, u32[]{:S(2)}) async-start(bf16[16,8,1536]{2,1,0:T(8,128)(2,1)} %fold.1), calls=%async_computation | async-start | bytes 786432 | tf_op jit(solution)/shard_map/all_to_all | solution.py:243
  9.3 2.0 %copy-start = (bf16[3,192,3072]{2,1,0:T(8,128)(2,1)S(1)}, bf16[3,192,3072]{2,1,0:T(8,128)(2,1)}, u32[]{:S(2)}) copy-start(bf16[3,192,3072]{2,1,0:T(8,128)(2,1)} %w_hbm.1) | copy-start | bytes 10616836
  11.3 0.7 copy-start.3
  12.0 0.7 copy-start.5
  12.7 0.7 copy-start.6
  17.3 8.8 %collective-permute-start.2 = (bf16[8,1536]{1,0:T(8,128)(2,1)S(1)}, bf16[8,1536]{1,0:T(8,128)(2,1)S(1)}, u32[]{:S(2)}, u32[]{:S(2)}) collective-permute-start(bf16[8,1536]{1,0:T(8,128)(2,1)S(1)} %slice_bitcast_fusion), channel_id=1, source_target_pairs={{16,48},{48,80},{80,112},{112,144},{144,176},{176,208},{208,240},{... | collective-permute-start | bytes 73736 | tf_op jit(solution)/shard_map/ppermute | solution.py:263
  21.1 5.0 %collective-permute-start.1 = (bf16[8,1536]{1,0:T(8,128)(2,1)S(1)}, bf16[8,1536]{1,0:T(8,128)(2,1)S(1)}, u32[]{:S(2)}, u32[]{:S(2)}) collective-permute-start(bf16[8,1536]{1,0:T(8,128)(2,1)S(1)} %slice_bitcast_fusion), channel_id=1, source_target_pairs={{16,32},{48,64},{80,96},{112,128},{144,160},{176,192},{208,224},{2... | collective-permute-start | bytes 73736 | tf_op jit(solution)/shard_map/ppermute | solution.py:262
  24.1 3.6 %collective-permute-start = (bf16[16,8,1536]{2,1,0:T(8,128)(2,1)S(1)}, bf16[16,8,1536]{2,1,0:T(8,128)(2,1)S(1)}, u32[]{:S(2)}, u32[]{:S(2)}) collective-permute-start(bf16[16,8,1536]{2,1,0:T(8,128)(2,1)S(1)} %all-to-all-done), channel_id=1, source_target_pairs={{0,16},{16,0},{32,48},{48,32},{64,80},{80,64},{96,112},{112,96},{1... | collective-permute-start | bytes 1179656 | tf_op jit(solution)/shard_map/ppermute | solution.py:260
  26.1 38.1 %copy-start.2 = (f32[2,3,64,64]{3,2,1,0:T(8,128)S(1)}, f32[2,3,64,64]{3,2,1,0:T(8,128)}, u32[]{:S(2)}) copy-start(f32[2,3,64,64]{3,2,1,0:T(8,128)} %init_ref.1) | copy-start | bytes 294916
  27.7 41.6 %copy-start.1 = (bf16[192,3072]{1,0:T(8,128)(2,1)S(1)}, bf16[192,3072]{1,0:T(8,128)(2,1)}, u32[]{:S(2)}) copy-start(bf16[192,3072]{1,0:T(8,128)(2,1)} %w_ref.1) | copy-start | bytes 3538948
  66.2 3.1 %collective-permute-start.3 = (f32[128,128]{1,0:T(8,128)S(1)}, f32[128,128]{1,0:T(8,128)S(1)}, u32[]{:S(2)}, u32[]{:S(2)}) collective-permute-start(f32[128,128]{1,0:T(8,128)S(1)} %chain.1.mine_ref), channel_id=1, source_target_pairs={{0,16},{16,0},{32,48},{48,32},{64,80},{80,64},{96,112},{112,96},{1... | collective-permute-start | bytes 196616 | tf_op jit(solution)/shard_map/ppermute | solution.py:301

commit v7 on v6

--- a/solution.py
+++ b/solution.py
@@ -162,19 +162,35 @@
     for way in range(2):
         shared = init_ref[way, 1, pl.ds(pl.multiple_of(32 * role, 32), 32), :]
         states.append([init_ref[way, 2 * role], shared])
-    for i in range(chips - 1):
+    def fetched(i, way):
+        j = i if way == 0 else chips - 1 - i
+        live = (j < chip) if way == 0 else (j > chip)
+        block = jnp.where(live, maps_ref[j].astype(F32), 0.0)
+        at = 64 + 48 * way
+        b0 = cat([block[at:at + 48, 0:64], block[at:at + 16, 64:128]], 0)
+        return [(block[0:64, 0:64], b0), (block[0:64, 64:128], block[at + 16:at + 48, 64:128])]
+
+    first = chips // 2
+    later = [None, None]
+    for i in range(first):
         for way in range(2):
-            j = i if way == 0 else chips - 1 - i
-            live = (j < chip) if way == 0 else (j > chip)
-            block = jnp.where(live, maps_ref[j].astype(F32), 0.0)
-            whole, shared = states[way]
-            at = 64 + 48 * way
-            steps = block[0:64].astype(BF16)
-            b0 = cat([block[at:at + 48, 0:64], block[at:at + 16, 64:128]], 0)
-            b1 = block[at + 16:at + 48, 64:128]
-            new0 = (whole + b0) + mm(whole.astype(BF16), steps[:, 0:64], 1, way)
-            new1 = (shared + b1) + mm(shared.astype(BF16), steps[:, 64:128], 1, way)
-            states[way] = [new0, new1]
+            near = fetched(i, way)
+            states[way] = [
+                (w + off) + mm(w.astype(BF16), step.astype(BF16), 1, way) for w, (step, off) in zip(states[way], near)
+            ]
+            if first + i < chips - 1:
+                far = fetched(first + i, way)
+                fresh = [cat([step if way == 0 else step.T, off], 0) for step, off in far]
+                if later[way] is None:
+                    later[way] = fresh
+                else:
+                    later[way] = [
+                        (x + f) + mm(x.astype(BF16), step.astype(BF16), 1, way) for x, f, (step, off) in zip(later[way], fresh, far)
+                    ]
+    for way in range(2):
+        states[way] = [
+            (w + x[64:]) + mm(w.astype(BF16), x[0:64].astype(BF16)) for w, x in zip(states[way], later[way])
+        ]
     sums = None
     for way in range(2):
         whole = mm(states[way][0].astype(BF16), qeff_ref[way, 0:64, :]) + oeff_ref[way, 0:64, :]

time: 83.6 us -> 83.7 us (level)
  no operation moved by 1% of the time
where the time goes in v7:
time: 83.7 us; the launch traced here: 83.2 us
  blocking collectives  46.6 us (56%)
  starting transfers between devices  18.4 us (22%)
  Pallas kernels  6.98 us (8%)
  waiting for transfers between devices  6.32 us (8%)
  local copies, waits for them, and re-layouts  4.83 us (6%)
    all_gather x1, blocking collectives, shards(): received = lax.all_gather(send, 'seq', axis_index_groups=groups)  34 us
    all_to_all x1, blocking collectives, shards(): parts = lax.all_to_all(partial.reshape(n_head, 8, half), 'head', 0, 0)  12.6 us
    all_to_all x1, starting transfers between devices, shards(): own = lax.all_to_all(folded, 'head', 0, 0)  7.6 us
    unnamed x14, local copies, waits for them, and re-layouts  4.83 us
    ppermute x1, starting transfers between devices, shards(): lax.ppermute(tail, 'seq', [(i, i + 2) for i in range(1, n_seq - 2, 2)])  3.79 us
    all_to_all x1, waiting for transfers between devices, shards(): own = lax.all_to_all(folded, 'head', 0, 0)  3.59 us
    ppermute x1, starting transfers between devices, shards(): lax.ppermute(tail, 'seq', [(i, i + 1) for i in range(1, n_seq - 1, 2)])  3.06 us
    pallas_call x1, Pallas kernels, shards(): pl.pallas_call(local_kernel, out_shape=(jax.ShapeDtypeStruct((160, 128),...  2.44 us
  transfers between devices with their start and end apart: 5, of which 3 were waited for; matrix products, arithmetic and copies ran while one was open for 0% of the time, Pallas kernels for 0%

profile of v7, /device:TPU:1, one launch (start us, length us, event | category | flops | bytes accessed | tf_op | source)
XLA Modules:
  0.0 83.2 jit_solution(18043062705264323425)
XLA Ops:
  0.0 0.7 copy-done.4
  0.7 0.9 %fold.1 = bf16[16,8,1536]{2,1,0:T(8,128)(2,1)} custom-call(bf16[4,3072]{1,0:T(4,128)(2,1)S(1)} %copy-done.4), custom_call_target="tpu_custom_call" | custom-call | tf_op jit(solution)/shard_map/fold/pallas_call | solution.py:246
  1.6 7.6 %all-to-all-start = ((bf16[16,8,1536]{2,1,0:T(8,128)(2,1)}), bf16[16,8,1536]{2,1,0:T(8,128)(2,1)S(1)}, u32[]{:S(2)}, u32[]{:S(2)}) async-start(bf16[16,8,1536]{2,1,0:T(8,128)(2,1)} %fold.1), calls=%async_computation | async-start | bytes 786432 | tf_op jit(solution)/shard_map/all_to_all | solution.py:259
  9.3 0.0 copy-start
  9.3 2.0 %copy-done = bf16[3,192,3072]{2,1,0:T(8,128)(2,1)S(1)} copy-done((bf16[3,192,3072]{2,1,0:T(8,128)(2,1)S(1)}, bf16[3,192,3072]{2,1,0:T(8,128)(2,1)}, u32[]{:S(2)}) %copy-start) | copy-done | bytes 3538968
  11.3 0.7 copy-done.3
  12.0 0.7 copy-done.5
  12.7 0.7 copy-done.6
  13.3 0.3 prepare.1
  13.7 3.6 %all-to-all-done = bf16[16,8,1536]{2,1,0:T(8,128)(2,1)S(1)} async-done(((bf16[16,8,1536]{2,1,0:T(8,128)(2,1)}), bf16[16,8,1536]{2,1,0:T(8,128)(2,1)S(1)}, u32[]{:S(2)}, u32[]{:S(2)}) %all-to-all-start) | async-done | bytes 393248 | tf_op jit(solution)/shard_map/all_to_all | solution.py:259
  17.3 3.8 %collective-permute-start.2 = (bf16[8,1536]{1,0:T(8,128)(2,1)S(1)}, bf16[8,1536]{1,0:T(8,128)(2,1)S(1)}, u32[]{:S(2)}, u32[]{:S(2)}) collective-permute-start(bf16[8,1536]{1,0:T(8,128)(2,1)S(1)} %slice_bitcast_fusion), channel_id=1, source_target_pairs={{16,48},{48,80},{80,112},{112,144},{144,176},{176,208},{208,240},{... | collective-permute-start | bytes 73736 | tf_op jit(solution)/shard_map/ppermute | solution.py:279
  21.1 3.1 %collective-permute-start.1 = (bf16[8,1536]{1,0:T(8,128)(2,1)S(1)}, bf16[8,1536]{1,0:T(8,128)(2,1)S(1)}, u32[]{:S(2)}, u32[]{:S(2)}) collective-permute-start(bf16[8,1536]{1,0:T(8,128)(2,1)S(1)} %slice_bitcast_fusion), channel_id=1, source_target_pairs={{16,32},{48,64},{80,96},{112,128},{144,160},{176,192},{208,224},{2... | collective-permute-start | bytes 73736 | tf_op jit(solution)/shard_map/ppermute | solution.py:278
  24.1 1.9 %collective-permute-start = (bf16[16,8,1536]{2,1,0:T(8,128)(2,1)S(1)}, bf16[16,8,1536]{2,1,0:T(8,128)(2,1)S(1)}, u32[]{:S(2)}, u32[]{:S(2)}) collective-permute-start(bf16[16,8,1536]{2,1,0:T(8,128)(2,1)S(1)} %all-to-all-done), channel_id=1, source_target_pairs={{0,16},{16,0},{32,48},{48,32},{64,80},{80,64},{96,112},{112,96},{1... | collective-permute-start | bytes 1179656 | tf_op jit(solution)/shard_map/ppermute | solution.py:276
  26.1 0.0 collective-permute-done.2.halo1_ref
  26.1 0.0 copy-start.2
  26.1 1.6 %collective-permute-done = bf16[16,8,1536]{2,1,0:T(8,128)(2,1)S(1)} collective-permute-done((bf16[16,8,1536]{2,1,0:T(8,128)(2,1)S(1)}, bf16[16,8,1536]{2,1,0:T(8,128)(2,1)S(1)}, u32[]{:S(2)}, u32[]{:S(2)}) %collective-permute-start) | collective-permute-done | bytes 393248 | tf_op jit(solution)/shard_map/ppermute | solution.py:276
  27.7 2.4 %local.1 = (bf16[160,128]{1,0:T(8,128)(2,1)S(1)}, bf16[2,128,128]{2,1,0:T(8,128)(2,1)S(1)}, f32[2,96,128]{2,1,0:T(8,128)S(1)}) custom-call(bf16[128,1536]{1,0:T(8,128)(2,1)S(1)} %bitcast.8, bf16[128,1536]{1,0:T(8,128)(2,1)S(1)} %bitcast.10, bf16[16,3072]{1,0:T(8,128)(2,1)S(1)} %tails.1.tail_ref, bf16[3,128,3072]{2,1,0:T(8,128)(2,1)S(1)} %get-tuple-element.16.w_ref, ...), custom_call_target="tpu_custom_call" | custom-call | tf_op jit(solution)/shard_map/local/pallas_call | solution.py:290
  30.2 34.0 %all-gather = bf16[2560,128]{1,0:T(8,128)(2,1)S(1)} all-gather(bf16[160,128]{1,0:T(8,128)(2,1)S(1)} %get-tuple-element.20), channel_id=2, replica_groups={{0,48,64,112,128,176,192,240,256,304,320,368,384,432,448,496},{16,32,80..., dimensions={0}, use_global_device_ids=true | all-gather | bytes 696320 | tf_op jit(solution)/shard_map/all_gather | solution.py:308
  64.2 2.0 %chain.1.mine_ref = f32[128,128]{1,0:T(8,128)S(1)} custom-call(bf16[16,160,128]{2,1,0:T(8,128)(2,1)S(1)} %bitcast.7, bf16[2,128,128]{2,1,0:T(8,128)(2,1)S(1)} %get-tuple-element.21.qeff_ref, f32[2,96,128]{2,1,0:T(8,128)S(1)} %get-tuple-element.22.oeff_ref, f32[2,3,64,64]{3,2,1,0:T(8,128)S(1)} %copy-done.2), custom_call_target="tpu_custom_call" | custom-call | tf_op jit(solution)/shard_map/chain/pallas_call | solution.py:309
  66.2 2.0 %collective-permute-start.3 = (f32[128,128]{1,0:T(8,128)S(1)}, f32[128,128]{1,0:T(8,128)S(1)}, u32[]{:S(2)}, u32[]{:S(2)}) collective-permute-start(f32[128,128]{1,0:T(8,128)S(1)} %chain.1.mine_ref), channel_id=1, source_target_pairs={{0,16},{16,0},{32,48},{48,32},{64,80},{80,64},{96,112},{112,96},{1... | collective-permute-start | bytes 196616 | tf_op jit(solution)/shard_map/ppermute | solution.py:317
  68.3 1.1 %collective-permute-done.3.mate_ref = f32[128,128]{1,0:T(8,128)S(1)} collective-permute-done((f32[128,128]{1,0:T(8,128)S(1)}, f32[128,128]{1,0:T(8,128)S(1)}, u32[]{:S(2)}, u32[]{:S(2)}) %collective-permute-start.3) | collective-permute-done | bytes 65568 | tf_op jit(solution)/shard_map/ppermute | solution.py:317
  69.4 0.6 output.1
  70.0 12.6 %all_to_all.10.parts_ref = bf16[16,8,1536]{2,1,0:T(8,128)(2,1)S(1)} all-to-all(bf16[16,8,1536]{2,1,0:T(8,128)(2,1)S(1)} %bitcast.9), channel_id=1, replica_groups=mesh['seq'=32,'head'=16] {'head'}, dimensions={0} | all-to-all | bytes 786432 | tf_op jit(solution)/shard_map/all_to_all | solution.py:326
  82.5 0.7 total.1
  (10 shorter events, 0.1 us)
Async XLA Ops:
  0.0 0.7 copy-start.4
  1.6 15.6 %all-to-all-start = ((bf16[16,8,1536]{2,1,0:T(8,128)(2,1)}), bf16[16,8,1536]{2,1,0:T(8,128)(2,1)S(1)}, u32[]{:S(2)}, u32[]{:S(2)}) async-start(bf16[16,8,1536]{2,1,0:T(8,128)(2,1)} %fold.1), calls=%async_computation | async-start | bytes 786432 | tf_op jit(solution)/shard_map/all_to_all | solution.py:259
  9.3 2.0 %copy-start = (bf16[3,192,3072]{2,1,0:T(8,128)(2,1)S(1)}, bf16[3,192,3072]{2,1,0:T(8,128)(2,1)}, u32[]{:S(2)}) copy-start(bf16[3,192,3072]{2,1,0:T(8,128)(2,1)} %w_hbm.1) | copy-start | bytes 10616836
  11.3 0.7 copy-start.3
  12.0 0.7 copy-start.5
  12.7 0.7 copy-start.6
  17.3 8.8 %collective-permute-start.2 = (bf16[8,1536]{1,0:T(8,128)(2,1)S(1)}, bf16[8,1536]{1,0:T(8,128)(2,1)S(1)}, u32[]{:S(2)}, u32[]{:S(2)}) collective-permute-start(bf16[8,1536]{1,0:T(8,128)(2,1)S(1)} %slice_bitcast_fusion), channel_id=1, source_target_pairs={{16,48},{48,80},{80,112},{112,144},{144,176},{176,208},{208,240},{... | collective-permute-start | bytes 73736 | tf_op jit(solution)/shard_map/ppermute | solution.py:279
  21.1 5.0 %collective-permute-start.1 = (bf16[8,1536]{1,0:T(8,128)(2,1)S(1)}, bf16[8,1536]{1,0:T(8,128)(2,1)S(1)}, u32[]{:S(2)}, u32[]{:S(2)}) collective-permute-start(bf16[8,1536]{1,0:T(8,128)(2,1)S(1)} %slice_bitcast_fusion), channel_id=1, source_target_pairs={{16,32},{48,64},{80,96},{112,128},{144,160},{176,192},{208,224},{2... | collective-permute-start | bytes 73736 | tf_op jit(solution)/shard_map/ppermute | solution.py:278
  24.1 3.6 %collective-permute-start = (bf16[16,8,1536]{2,1,0:T(8,128)(2,1)S(1)}, bf16[16,8,1536]{2,1,0:T(8,128)(2,1)S(1)}, u32[]{:S(2)}, u32[]{:S(2)}) collective-permute-start(bf16[16,8,1536]{2,1,0:T(8,128)(2,1)S(1)} %all-to-all-done), channel_id=1, source_target_pairs={{0,16},{16,0},{32,48},{48,32},{64,80},{80,64},{96,112},{112,96},{1... | collective-permute-start | bytes 1179656 | tf_op jit(solution)/shard_map/ppermute | solution.py:276
  26.1 38.1 %copy-start.2 = (f32[2,3,64,64]{3,2,1,0:T(8,128)S(1)}, f32[2,3,64,64]{3,2,1,0:T(8,128)}, u32[]{:S(2)}) copy-start(f32[2,3,64,64]{3,2,1,0:T(8,128)} %init_ref.1) | copy-start | bytes 294916
  27.7 41.6 %copy-start.1 = (bf16[192,3072]{1,0:T(8,128)(2,1)S(1)}, bf16[192,3072]{1,0:T(8,128)(2,1)}, u32[]{:S(2)}) copy-start(bf16[192,3072]{1,0:T(8,128)(2,1)} %w_ref.1) | copy-start | bytes 3538948
  66.2 3.1 %collective-permute-start.3 = (f32[128,128]{1,0:T(8,128)S(1)}, f32[128,128]{1,0:T(8,128)S(1)}, u32[]{:S(2)}, u32[]{:S(2)}) collective-permute-start(f32[128,128]{1,0:T(8,128)S(1)} %chain.1.mine_ref), channel_id=1, source_target_pairs={{0,16},{16,0},{32,48},{48,32},{64,80},{80,64},{96,112},{112,96},{1... | collective-permute-start | bytes 196616 | tf_op jit(solution)/shard_map/ppermute | solution.py:317

commit v8 on v6

--- a/solution.py
+++ b/solution.py
@@ -135,9 +135,9 @@
     t1 = [eye - u[i] + u2[i] - u3[i] for i in two]
     t = [t1[i] + mm(t1[i].astype(BF16), u4[i]) for i in two]
     rev = [t[i].T * rate[i] for i in two]
-    ways = [[x.T.astype(BF16) for x in rev], [x.astype(BF16) for x in rev]]
+    revb = [x.astype(BF16) for x in rev]
     seen = [[jnp.where(mask, grams[i][:, 128:256], 0.0).astype(BF16) for i in two] for mask in (dst >= src, dst <= src)]
-    solved = [[mm(ways[w][i], cat([seen[w][i], kt[i]], 1)).astype(BF16) for i in two] for w in two]
+    solved = [[mm(revb[i], cat([seen[w][i], kt[i]], 1), w, 0).astype(BF16) for i in two] for w in two]
     stacked = [cat([kb[i], v[i].astype(BF16)], 0) for i in two]
     both = [[mm(stacked[i], solved[w][i]) for i in two] for w in two]
     for w in two:

time: 83.6 us -> 83.6 us (level)
  no operation moved by 1% of the time
where the time goes in v8:
time: 83.6 us; the launch traced here: 83.1 us
  blocking collectives  46.5 us (56%)
  starting transfers between devices  18.4 us (22%)
  Pallas kernels  6.91 us (8%)
  waiting for transfers between devices  6.32 us (8%)
  local copies, waits for them, and re-layouts  4.83 us (6%)
    all_gather x1, blocking collectives, shards(): received = lax.all_gather(send, 'seq', axis_index_groups=groups)  34 us
    all_to_all x1, blocking collectives, shards(): parts = lax.all_to_all(partial.reshape(n_head, 8, half), 'head', 0, 0)  12.5 us
    all_to_all x1, starting transfers between devices, shards(): own = lax.all_to_all(folded, 'head', 0, 0)  7.6 us
    unnamed x14, local copies, waits for them, and re-layouts  4.83 us
    ppermute x1, starting transfers between devices, shards(): lax.ppermute(tail, 'seq', [(i, i + 2) for i in range(1, n_seq - 2, 2)])  3.79 us
    all_to_all x1, waiting for transfers between devices, shards(): own = lax.all_to_all(folded, 'head', 0, 0)  3.59 us
    ppermute x1, starting transfers between devices, shards(): lax.ppermute(tail, 'seq', [(i, i + 1) for i in range(1, n_seq - 1, 2)])  3.06 us
    pallas_call x1, Pallas kernels, shards(): pl.pallas_call(local_kernel, out_shape=(jax.ShapeDtypeStruct((160, 128),...  2.44 us
  transfers between devices with their start and end apart: 5, of which 3 were waited for; matrix products, arithmetic and copies ran while one was open for 0% of the time, Pallas kernels for 0%

profile of v8, /device:TPU:1, one launch (start us, length us, event | category | flops | bytes accessed | tf_op | source)
XLA Modules:
  0.0 83.1 jit_solution(10088471347255782803)
XLA Ops:
  0.0 0.7 copy-done.4
  0.7 0.9 %fold.1 = bf16[16,8,1536]{2,1,0:T(8,128)(2,1)} custom-call(bf16[4,3072]{1,0:T(4,128)(2,1)S(1)} %copy-done.4), custom_call_target="tpu_custom_call" | custom-call | tf_op jit(solution)/shard_map/fold/pallas_call | solution.py:230
  1.6 7.6 %all-to-all-start = ((bf16[16,8,1536]{2,1,0:T(8,128)(2,1)}), bf16[16,8,1536]{2,1,0:T(8,128)(2,1)S(1)}, u32[]{:S(2)}, u32[]{:S(2)}) async-start(bf16[16,8,1536]{2,1,0:T(8,128)(2,1)} %fold.1), calls=%async_computation | async-start | bytes 786432 | tf_op jit(solution)/shard_map/all_to_all | solution.py:243
  9.3 0.0 copy-start
  9.3 2.0 %copy-done = bf16[3,192,3072]{2,1,0:T(8,128)(2,1)S(1)} copy-done((bf16[3,192,3072]{2,1,0:T(8,128)(2,1)S(1)}, bf16[3,192,3072]{2,1,0:T(8,128)(2,1)}, u32[]{:S(2)}) %copy-start) | copy-done | bytes 3538968
  11.3 0.7 copy-done.3
  12.0 0.7 copy-done.5
  12.7 0.7 copy-done.6
  13.3 0.3 prepare.1
  13.7 3.6 %all-to-all-done = bf16[16,8,1536]{2,1,0:T(8,128)(2,1)S(1)} async-done(((bf16[16,8,1536]{2,1,0:T(8,128)(2,1)}), bf16[16,8,1536]{2,1,0:T(8,128)(2,1)S(1)}, u32[]{:S(2)}, u32[]{:S(2)}) %all-to-all-start) | async-done | bytes 393248 | tf_op jit(solution)/shard_map/all_to_all | solution.py:243
  17.3 3.8 %collective-permute-start.2 = (bf16[8,1536]{1,0:T(8,128)(2,1)S(1)}, bf16[8,1536]{1,0:T(8,128)(2,1)S(1)}, u32[]{:S(2)}, u32[]{:S(2)}) collective-permute-start(bf16[8,1536]{1,0:T(8,128)(2,1)S(1)} %slice_bitcast_fusion), channel_id=1, source_target_pairs={{16,48},{48,80},{80,112},{112,144},{144,176},{176,208},{208,240},{... | collective-permute-start | bytes 73736 | tf_op jit(solution)/shard_map/ppermute | solution.py:263
  21.1 3.1 %collective-permute-start.1 = (bf16[8,1536]{1,0:T(8,128)(2,1)S(1)}, bf16[8,1536]{1,0:T(8,128)(2,1)S(1)}, u32[]{:S(2)}, u32[]{:S(2)}) collective-permute-start(bf16[8,1536]{1,0:T(8,128)(2,1)S(1)} %slice_bitcast_fusion), channel_id=1, source_target_pairs={{16,32},{48,64},{80,96},{112,128},{144,160},{176,192},{208,224},{2... | collective-permute-start | bytes 73736 | tf_op jit(solution)/shard_map/ppermute | solution.py:262
  24.1 1.9 %collective-permute-start = (bf16[16,8,1536]{2,1,0:T(8,128)(2,1)S(1)}, bf16[16,8,1536]{2,1,0:T(8,128)(2,1)S(1)}, u32[]{:S(2)}, u32[]{:S(2)}) collective-permute-start(bf16[16,8,1536]{2,1,0:T(8,128)(2,1)S(1)} %all-to-all-done), channel_id=1, source_target_pairs={{0,16},{16,0},{32,48},{48,32},{64,80},{80,64},{96,112},{112,96},{1... | collective-permute-start | bytes 1179656 | tf_op jit(solution)/shard_map/ppermute | solution.py:260
  26.1 0.0 collective-permute-done.2.halo1_ref
  26.1 0.0 copy-start.2
  26.1 1.6 %collective-permute-done = bf16[16,8,1536]{2,1,0:T(8,128)(2,1)S(1)} collective-permute-done((bf16[16,8,1536]{2,1,0:T(8,128)(2,1)S(1)}, bf16[16,8,1536]{2,1,0:T(8,128)(2,1)S(1)}, u32[]{:S(2)}, u32[]{:S(2)}) %collective-permute-start) | collective-permute-done | bytes 393248 | tf_op jit(solution)/shard_map/ppermute | solution.py:260
  27.7 2.4 %local.1 = (bf16[160,128]{1,0:T(8,128)(2,1)S(1)}, bf16[2,128,128]{2,1,0:T(8,128)(2,1)S(1)}, f32[2,96,128]{2,1,0:T(8,128)S(1)}) custom-call(bf16[128,1536]{1,0:T(8,128)(2,1)S(1)} %bitcast.8, bf16[128,1536]{1,0:T(8,128)(2,1)S(1)} %bitcast.10, bf16[16,3072]{1,0:T(8,128)(2,1)S(1)} %tails.1.tail_ref, bf16[3,128,3072]{2,1,0:T(8,128)(2,1)S(1)} %get-tuple-element.16.w_ref, ...), custom_call_target="tpu_custom_call" | custom-call | tf_op jit(solution)/shard_map/local/pallas_call | solution.py:274
  30.2 34.0 %all-gather = bf16[2560,128]{1,0:T(8,128)(2,1)S(1)} all-gather(bf16[160,128]{1,0:T(8,128)(2,1)S(1)} %get-tuple-element.20), channel_id=2, replica_groups={{0,48,64,112,128,176,192,240,256,304,320,368,384,432,448,496},{16,32,80..., dimensions={0}, use_global_device_ids=true | all-gather | bytes 696320 | tf_op jit(solution)/shard_map/all_gather | solution.py:292
  64.2 2.0 %chain.1.mine_ref = f32[128,128]{1,0:T(8,128)S(1)} custom-call(bf16[16,160,128]{2,1,0:T(8,128)(2,1)S(1)} %bitcast.7, bf16[2,128,128]{2,1,0:T(8,128)(2,1)S(1)} %get-tuple-element.21.qeff_ref, f32[2,96,128]{2,1,0:T(8,128)S(1)} %get-tuple-element.22.oeff_ref, f32[2,3,64,64]{3,2,1,0:T(8,128)S(1)} %copy-done.2), custom_call_target="tpu_custom_call" | custom-call | tf_op jit(solution)/shard_map/chain/pallas_call | solution.py:293
  66.2 2.0 %collective-permute-start.3 = (f32[128,128]{1,0:T(8,128)S(1)}, f32[128,128]{1,0:T(8,128)S(1)}, u32[]{:S(2)}, u32[]{:S(2)}) collective-permute-start(f32[128,128]{1,0:T(8,128)S(1)} %chain.1.mine_ref), channel_id=1, source_target_pairs={{0,16},{16,0},{32,48},{48,32},{64,80},{80,64},{96,112},{112,96},{1... | collective-permute-start | bytes 196616 | tf_op jit(solution)/shard_map/ppermute | solution.py:301
  68.2 1.1 %collective-permute-done.3.mate_ref = f32[128,128]{1,0:T(8,128)S(1)} collective-permute-done((f32[128,128]{1,0:T(8,128)S(1)}, f32[128,128]{1,0:T(8,128)S(1)}, u32[]{:S(2)}, u32[]{:S(2)}) %collective-permute-start.3) | collective-permute-done | bytes 65568 | tf_op jit(solution)/shard_map/ppermute | solution.py:301
  69.3 0.6 output.1
  69.9 12.5 %all_to_all.10.parts_ref = bf16[16,8,1536]{2,1,0:T(8,128)(2,1)S(1)} all-to-all(bf16[16,8,1536]{2,1,0:T(8,128)(2,1)S(1)} %bitcast.9), channel_id=1, replica_groups=mesh['seq'=32,'head'=16] {'head'}, dimensions={0} | all-to-all | bytes 786432 | tf_op jit(solution)/shard_map/all_to_all | solution.py:310
  82.4 0.7 total.1
  (10 shorter events, 0.1 us)
Async XLA Ops:
  0.0 0.7 copy-start.4
  1.6 15.6 %all-to-all-start = ((bf16[16,8,1536]{2,1,0:T(8,128)(2,1)}), bf16[16,8,1536]{2,1,0:T(8,128)(2,1)S(1)}, u32[]{:S(2)}, u32[]{:S(2)}) async-start(bf16[16,8,1536]{2,1,0:T(8,128)(2,1)} %fold.1), calls=%async_computation | async-start | bytes 786432 | tf_op jit(solution)/shard_map/all_to_all | solution.py:243
  9.3 2.0 %copy-start = (bf16[3,192,3072]{2,1,0:T(8,128)(2,1)S(1)}, bf16[3,192,3072]{2,1,0:T(8,128)(2,1)}, u32[]{:S(2)}) copy-start(bf16[3,192,3072]{2,1,0:T(8,128)(2,1)} %w_hbm.1) | copy-start | bytes 10616836
  11.3 0.7 copy-start.3
  12.0 0.7 copy-start.5
  12.7 0.7 copy-start.6
  17.3 8.8 %collective-permute-start.2 = (bf16[8,1536]{1,0:T(8,128)(2,1)S(1)}, bf16[8,1536]{1,0:T(8,128)(2,1)S(1)}, u32[]{:S(2)}, u32[]{:S(2)}) collective-permute-start(bf16[8,1536]{1,0:T(8,128)(2,1)S(1)} %slice_bitcast_fusion), channel_id=1, source_target_pairs={{16,48},{48,80},{80,112},{112,144},{144,176},{176,208},{208,240},{... | collective-permute-start | bytes 73736 | tf_op jit(solution)/shard_map/ppermute | solution.py:263
  21.1 5.0 %collective-permute-start.1 = (bf16[8,1536]{1,0:T(8,128)(2,1)S(1)}, bf16[8,1536]{1,0:T(8,128)(2,1)S(1)}, u32[]{:S(2)}, u32[]{:S(2)}) collective-permute-start(bf16[8,1536]{1,0:T(8,128)(2,1)S(1)} %slice_bitcast_fusion), channel_id=1, source_target_pairs={{16,32},{48,64},{80,96},{112,128},{144,160},{176,192},{208,224},{2... | collective-permute-start | bytes 73736 | tf_op jit(solution)/shard_map/ppermute | solution.py:262
  24.1 3.6 %collective-permute-start = (bf16[16,8,1536]{2,1,0:T(8,128)(2,1)S(1)}, bf16[16,8,1536]{2,1,0:T(8,128)(2,1)S(1)}, u32[]{:S(2)}, u32[]{:S(2)}) collective-permute-start(bf16[16,8,1536]{2,1,0:T(8,128)(2,1)S(1)} %all-to-all-done), channel_id=1, source_target_pairs={{0,16},{16,0},{32,48},{48,32},{64,80},{80,64},{96,112},{112,96},{1... | collective-permute-start | bytes 1179656 | tf_op jit(solution)/shard_map/ppermute | solution.py:260
  26.1 38.1 %copy-start.2 = (f32[2,3,64,64]{3,2,1,0:T(8,128)S(1)}, f32[2,3,64,64]{3,2,1,0:T(8,128)}, u32[]{:S(2)}) copy-start(f32[2,3,64,64]{3,2,1,0:T(8,128)} %init_ref.1) | copy-start | bytes 294916
  27.7 41.6 %copy-start.1 = (bf16[192,3072]{1,0:T(8,128)(2,1)S(1)}, bf16[192,3072]{1,0:T(8,128)(2,1)}, u32[]{:S(2)}) copy-start(bf16[192,3072]{1,0:T(8,128)(2,1)} %w_ref.1) | copy-start | bytes 3538948
  66.2 3.1 %collective-permute-start.3 = (f32[128,128]{1,0:T(8,128)S(1)}, f32[128,128]{1,0:T(8,128)S(1)}, u32[]{:S(2)}, u32[]{:S(2)}) collective-permute-start(f32[128,128]{1,0:T(8,128)S(1)} %chain.1.mine_ref), channel_id=1, source_target_pairs={{0,16},{16,0},{32,48},{48,32},{64,80},{80,64},{96,112},{112,96},{1... | collective-permute-start | bytes 196616 | tf_op jit(solution)/shard_map/ppermute | solution.py:301
